TPU v7x, 32 devices: a whole 2x2x4 slice. The times are simulated.
32 devices in a mesh: region: 16 (over z, x, core), head: 2 (over y).
Axes of the slice: x: 2, y: 2, z: 4, core: 2. Of those that a mesh axis runs over, the one named last changes fastest.
Arguments:
- points: bfloat16 [16384, 512], P('region'), may hold values from -6 to 6
- ln_gain: float32 [512], replicated, may hold values from 0.5 to 1.5
- ln_bias: float32 [512], replicated, may hold values from -3 to 3
- w_qkv: bfloat16 [512, 3, 512], P(None, None, 'head')
- b_qkv: float32 [3, 512], P(None, 'head'), may hold values from -3 to 3
- w_proj: bfloat16 [512, 512], P('head'), may hold values from -0.25 to 0.25
- b_proj: float32 [512], replicated, may hold values from -3 to 3
- counts: int32 [512], replicated, may hold values from 1 to 32
- hilbert_pos: int32 [512], replicated, may hold values from 0 to 511, as said below
Outputs:
- update: bfloat16 [16384, 512], P(('region', 'head'))
Inputs may be any that keep to these rules, and one draw needn't show every extreme that they name: `hilbert_pos`: a permutation; the 32 z-order blocks of one region index land on exactly 8 region indices in Hilbert order, exactly 4 on each (position // 32 is the index).
All inputs are finite; a program needn't handle non-finite values.
Results may differ from a plain program's by a relative error of at most 0.014.
The roundings to bfloat16 on the way count: a program that leaves them out, or rounds other values in their place, can miss the bound.
Values may be sent and summed in bfloat16 or wider, within the bound.
A program may use at most 64 MiB of HBM per device.

v0:
```python
import functools

import jax
import jax.numpy as jnp
from jax import lax
from jax.experimental import pallas as pl
from jax.experimental.pallas import tpu as pltpu
from jax.sharding import PartitionSpec as P

HD = 16
PATCH = 1024
BS = 32
LANES = 128

epsilon = 1e-05
MESH = pl.DeviceIdType.MESH


def pack_kernel(total, parts, tile, pack_ref, head_ref, x_ref, gain_ref, bias_ref, out_ref, own):
    rows, depth = x_ref.shape
    width = depth // parts
    h = head_ref[0]

    def pick(value):
        chosen = value[:, :width]
        for part in range(1, parts):
            chosen = jnp.where(h == part, value[:, part * width:(part + 1) * width], chosen)
        return chosen

    gain = pick(gain_ref[...])
    bias = pick(bias_ref[...])

    def normalize(i, carry):
        part = pl.ds(pl.multiple_of(i * tile, tile), tile)
        values = x_ref[part, :].astype(jnp.float32)
        centred = values - jnp.mean(values, axis=-1, keepdims=True)
        row_var = jnp.mean(centred * centred, axis=-1, keepdims=True)
        own[part, :] = (pick(centred) * lax.rsqrt(row_var + epsilon) * gain + bias).astype(
            jnp.bfloat16
        )
        return carry

    lax.fori_loop(0, rows // tile, normalize, 0)

    def pack(j, carry):
        source = pl.multiple_of(pack_ref[j] * BS, BS)
        out_ref[pl.ds(pl.multiple_of(j * BS, BS), BS), :] = own[pl.ds(source, BS), :]
        return carry

    lax.fori_loop(0, total, pack, 0, unroll=8)


def pack_blocks(points, ln_gain, ln_bias, head, pack_table, parts, tile=256):
    total = pack_table.shape[0]
    rows, depth = points.shape
    vmem = pl.BlockSpec(memory_space=pltpu.VMEM)
    smem = pl.BlockSpec(memory_space=pltpu.SMEM)
    return pl.pallas_call(
        functools.partial(pack_kernel, total, parts, tile),
        out_shape=jax.ShapeDtypeStruct((total * BS, depth // parts), jnp.bfloat16),
        in_specs=[smem, smem, vmem, vmem, vmem],
        out_specs=vmem,
        scratch_shapes=[pltpu.VMEM((rows, depth // parts), jnp.bfloat16)],
        name="pack",
    )(pack_table, head.reshape(1), points, ln_gain.reshape(1, -1), ln_bias.reshape(1, -1))


def exchange_kernel(
    regions, heads_axis, chunk,
    send, recv, own_sem, send_sem, recv_sem, fsend_sem, frecv_sem,
):
    r = lax.axis_index("region")
    h = lax.axis_index("head")

    barrier = pltpu.get_barrier_semaphore()

    def greet(d, carry):
        pl.semaphore_signal(
            barrier, inc=1, device_id={"region": lax.rem(r + d, regions)}, device_id_type=MESH
        )
        return carry

    lax.fori_loop(1, regions, greet, 0)
    for e in range(1, heads_axis):
        pl.semaphore_signal(
            barrier, inc=1, device_id={"head": lax.rem(h + e, heads_axis)}, device_id_type=MESH
        )
    pl.semaphore_wait(barrier, regions - 1 + heads_axis - 1)

    def rows(s):
        return pl.ds(pl.multiple_of(s * chunk, chunk), chunk)

    def to_region(t):
        return pltpu.make_async_remote_copy(
            src_ref=send.at[rows(t)],
            dst_ref=recv.at[h, rows(r)],
            send_sem=send_sem.at[t],
            recv_sem=recv_sem.at[r],
            device_id={"region": t},
            device_id_type=MESH,
        )

    def from_region(s):
        return pltpu.make_async_remote_copy(
            src_ref=send.at[rows(s)],
            dst_ref=recv.at[h, rows(s)],
            send_sem=send_sem.at[s],
            recv_sem=recv_sem.at[s],
            device_id={"region": s},
            device_id_type=MESH,
        )

    def to_head(e, s, source):
        return pltpu.make_async_remote_copy(
            src_ref=source,
            dst_ref=recv.at[h, rows(s)],
            send_sem=fsend_sem.at[e, s],
            recv_sem=frecv_sem.at[h, s],
            device_id={"head": lax.rem(h + e, heads_axis)},
            device_id_type=MESH,
        )

    def from_head(e, s):
        other = lax.rem(h + e, heads_axis)
        return pltpu.make_async_remote_copy(
            src_ref=recv.at[other, rows(s)],
            dst_ref=recv.at[other, rows(s)],
            send_sem=fsend_sem.at[e, s],
            recv_sem=frecv_sem.at[other, s],
            device_id={"head": other},
            device_id_type=MESH,
        )

    def push(d, carry):
        to_region(lax.rem(r + d, regions)).start()
        return carry

    own = pltpu.make_async_copy(send.at[rows(r)], recv.at[h, rows(r)], own_sem)
    own.start()
    for e in range(1, heads_axis):
        to_head(e, r, send.at[rows(r)]).start()
    lax.fori_loop(1, regions, push, 0)

    def relay(d, carry):
        s = lax.rem(r - d + regions, regions)
        from_region(s).wait_recv()
        for e in range(1, heads_axis):
            to_head(e, s, recv.at[h, rows(s)]).start()
        return carry

    lax.fori_loop(1, regions, relay, 0)
    own.wait()

    def finish(d, carry):
        s = lax.rem(r - d + regions, regions)
        for e in range(1, heads_axis):
            from_head(e, s).wait_recv()
            to_head(e, s, recv.at[h, rows(s)]).wait_send()
        return carry

    lax.fori_loop(0, regions, finish, 0)

    def drain(d, carry):
        from_region(lax.rem(r + d, regions)).wait_send()
        return carry

    lax.fori_loop(1, regions, drain, 0)


def exchange(packed, regions, heads_axis):
    rows, width = packed.shape
    return pl.pallas_call(
        functools.partial(exchange_kernel, regions, heads_axis, rows // regions),
        out_shape=jax.ShapeDtypeStruct((heads_axis, rows, width), jnp.bfloat16),
        in_specs=[pl.BlockSpec(memory_space=pltpu.VMEM)],
        out_specs=pl.BlockSpec(memory_space=pltpu.VMEM),
        scratch_shapes=[
            pltpu.SemaphoreType.DMA,
            pltpu.SemaphoreType.DMA((regions,)),
            pltpu.SemaphoreType.DMA((regions,)),
            pltpu.SemaphoreType.DMA((heads_axis, regions)),
            pltpu.SemaphoreType.DMA((heads_axis, regions)),
        ],
        compiler_params=pltpu.CompilerParams(collective_id=0, has_side_effects=True),
        name="exchange",
    )(packed)


def project_kernel(
    blocks, tile, slot_ref, count_ref, recv, valid_ref, w_ref, b_ref, out_ref, full
):
    parts, _, piece = recv.shape
    width = w_ref.shape[1] // 3
    row_index = lax.broadcasted_iota(jnp.int32, (BS, piece), 0)

    def unpack(t, carry):
        source = pl.multiple_of(slot_ref[t] * BS, BS)
        count = count_ref[t]
        for part in range(parts):
            block = recv[part, pl.ds(source, BS), :].astype(jnp.float32)
            block = jnp.where(row_index < count, block, block[0:1, :])
            full[pl.ds(pl.multiple_of(t * BS, BS), BS), part * piece:(part + 1) * piece] = (
                block.astype(jnp.bfloat16)
            )
        return carry

    def multiply(i, carry):
        first = i * (tile // BS)
        lax.fori_loop(0, tile // BS, lambda t, c: unpack(first + t, c), 0, unroll=4)
        part = pl.ds(pl.multiple_of(i * tile, tile), tile)
        for c in range(3):
            columns = slice(c * width, (c + 1) * width)
            summed = jnp.dot(full[part, :], w_ref[:, columns], preferred_element_type=jnp.float32)
            summed = summed + b_ref[:, columns]
            if c == 0:
                summed = summed * HD ** (-0.5)
            if c == 2:
                keep = valid_ref[part, :].astype(jnp.float32)
                keep = jnp.concatenate([keep] * (width // LANES), axis=1)
                summed = jnp.where(keep > 0, summed, 0.0)
            out_ref[part, columns] = summed.astype(jnp.bfloat16)
        return carry

    lax.fori_loop(0, blocks * BS // tile, multiply, 0)


def project(recv, slot_table, own_counts, valid, weight, bias, tile=256):
    blocks = slot_table.shape[0]
    vmem = pl.BlockSpec(memory_space=pltpu.VMEM)
    smem = pl.BlockSpec(memory_space=pltpu.SMEM)
    return pl.pallas_call(
        functools.partial(project_kernel, blocks, tile),
        out_shape=jax.ShapeDtypeStruct((blocks * BS, weight.shape[1]), jnp.bfloat16),
        in_specs=[smem, smem, vmem, vmem, vmem, vmem],
        out_specs=vmem,
        scratch_shapes=[pltpu.VMEM((blocks * BS, weight.shape[0]), jnp.bfloat16)],
        name="project",
    )(slot_table, own_counts, recv, valid, weight, bias.reshape(1, -1))


def over_heads(heads, tile, q_ref, keys, vals, acc, den, ahead, peaks_out=None, peaks_in=None):
    queries, width = q_ref.shape
    lane = lax.broadcasted_iota(jnp.int32, (1, LANES), 1)
    steps = queries // tile
    per = LANES // HD

    for c in range(width // LANES):
        columns = slice(c * LANES, (c + 1) * LANES)
        count = min(per, heads - c * per)
        trip_heads = 4 if count % 4 == 0 else 2

        def score(n, i):
            mine = (lane // HD == n).astype(jnp.float32).astype(jnp.bfloat16)
            return lax.dot_general(
                q_ref[i * tile:(i + 1) * tile, columns] * mine, keys[:, columns],
                (((1,), (1,)), ((), ())), preferred_element_type=jnp.float32,
            )

        ahead[0] = score(0, 0)

        def several(trip, carry):
            order = [(trip_heads * trip + u, i) for u in range(trip_heads) for i in range(steps)]
            after = order[1:] + [(jnp.minimum(trip_heads * (trip + 1), count - 1), 0)]
            for turn, (n, i) in enumerate(order):
                part = slice(i * tile, (i + 1) * tile)
                ahead[(turn + 1) % 2] = score(*after[turn])
                scores = ahead[turn % 2]
                peak = jnp.max(scores, axis=-1, keepdims=True)
                if peaks_in is not None:
                    old = jnp.sum(
                        jnp.where(lane == n + c * per, peaks_in[part, :], 0.0),
                        axis=-1, keepdims=True,
                    )
                    peak = jnp.maximum(peak, old)
                    keep = jnp.exp(old - peak)
                if peaks_out is not None:
                    peaks_out[part, :] = jnp.where(
                        lane == n + c * per, peak, peaks_out[part, :]
                    )
                expo = jnp.exp(scores - peak).astype(jnp.bfloat16)
                result = jnp.dot(expo, vals[c], preferred_element_type=jnp.float32)
                mine = lane // HD == n
                over, under = acc[part, columns], den[part, columns]
                top, low = result[:, :LANES], result[:, LANES:]
                if peaks_in is not None:
                    top, low = over * keep + top, under * keep + low
                acc[part, columns] = jnp.where(mine, top, over)
                den[part, columns] = jnp.where(mine, low, under)
            return carry

        lax.fori_loop(0, count // trip_heads, several, 0)


def finish_heads(acc, den, w_ref, out_ref):
    attended = (acc[...] / den[...]).astype(jnp.bfloat16)
    out_ref[...] = jnp.dot(attended, w_ref[...], preferred_element_type=jnp.float32).astype(
        jnp.bfloat16
    )


def fill_values(vals, v_ref, on_ref, first):
    count = v_ref.shape[0]
    for c in range(vals.shape[0]):
        vals[c, first:first + count, :LANES] = v_ref[:, c * LANES:(c + 1) * LANES]
        vals[c, first:first + count, LANES:] = on_ref[...]


def near_kernel(
    heads, tile, half_ref, q_ref, kn_ref, vn_ref, on_ref, acc, den, peaks, vals, ahead
):
    fill_values(vals, vn_ref, on_ref, 0)
    acc[...] = jnp.zeros_like(acc)
    den[...] = jnp.ones_like(den)
    peaks[...] = jnp.zeros_like(peaks)
    over_heads(heads, tile, q_ref, kn_ref, vals, acc, den, ahead, peaks_out=peaks)


def far_kernel(
    heads, tile, half_ref, q_ref, kf_ref, vf_ref, of_ref, w_ref, acc0, den0, peaks, out_ref,
    vals, acc, den, ahead,
):
    fill_values(vals, vf_ref, of_ref, 0)
    acc[...] = acc0[...]
    den[...] = den0[...]
    over_heads(heads, tile, q_ref, kf_ref, vals, acc, den, ahead, peaks_in=peaks)
    finish_heads(acc, den, w_ref, out_ref)


def attend_kernel(
    heads, tile,
    half_ref, q_ref, kn_ref, vn_ref, on_ref, kf_ref, vf_ref, of_ref, w_ref, out_ref,
    keys, vals, acc, den, ahead,
):
    near = kn_ref.shape[0]
    keys[:near, :] = kn_ref[...]
    keys[near:, :] = kf_ref[...]
    fill_values(vals, vn_ref, on_ref, 0)
    fill_values(vals, vf_ref, of_ref, near)
    acc[...] = jnp.zeros_like(acc)
    den[...] = jnp.ones_like(den)
    over_heads(heads, tile, q_ref, keys, vals, acc, den, ahead)
    finish_heads(acc, den, w_ref, out_ref)


def whole_block(*shape):
    return pl.BlockSpec(shape, lambda i, half: (0,) * len(shape))


def half_block(queries, width, column):
    return pl.BlockSpec((queries, width), lambda i, half: (half[0], column))


def attend_cost(heads, queries, keys, width):
    return pl.CostEstimate(
        flops=heads * queries * keys * width * 4,
        bytes_accessed=queries * width * 20,
        transcendentals=heads * queries * keys,
    )


def attend_near(half, qkv, valid, width, queries, heads, tile=512):
    return pl.pallas_call(
        functools.partial(near_kernel, heads, tile),
        out_shape=[
            jax.ShapeDtypeStruct((queries, width), jnp.float32),
            jax.ShapeDtypeStruct((queries, width), jnp.float32),
            jax.ShapeDtypeStruct((queries, LANES), jnp.float32),
        ],
        grid_spec=pltpu.PrefetchScalarGridSpec(
            num_scalar_prefetch=1,
            grid=(1,),
            in_specs=[half_block(queries, width, c) for c in range(3)]
            + [half_block(queries, LANES, 0)],
            out_specs=[
                whole_block(queries, width), whole_block(queries, width),
                whole_block(queries, LANES),
            ],
            scratch_shapes=[pltpu.VMEM((width // LANES, queries, 2 * LANES), jnp.bfloat16)]
            + [pltpu.VMEM((2, tile, queries), jnp.float32)],
        ),
        cost_estimate=attend_cost(heads, queries, queries, width),
        name="attend_near",
    )(half.reshape(1), qkv, qkv, qkv, valid)


def attend_far(half, qkv, far_kv, far_valid, w_proj, state, heads, tile=512):
    width, columns = w_proj.shape
    queries = far_kv.shape[0]
    return pl.pallas_call(
        functools.partial(far_kernel, heads, tile),
        out_shape=jax.ShapeDtypeStruct((queries, columns), jnp.bfloat16),
        grid_spec=pltpu.PrefetchScalarGridSpec(
            num_scalar_prefetch=1,
            grid=(1,),
            in_specs=[
                half_block(queries, width, 0),
                pl.BlockSpec((queries, width), lambda i, half: (0, 0)),
                pl.BlockSpec((queries, width), lambda i, half: (0, 1)),
                whole_block(queries, LANES),
                whole_block(width, columns),
                whole_block(queries, width), whole_block(queries, width),
                whole_block(queries, LANES),
            ],
            out_specs=whole_block(queries, columns),
            scratch_shapes=[pltpu.VMEM((width // LANES, queries, 2 * LANES), jnp.bfloat16)]
            + [pltpu.VMEM((queries, width), jnp.float32)] * 2
            + [pltpu.VMEM((2, tile, queries), jnp.float32)],
        ),
        cost_estimate=attend_cost(heads, queries, queries, width),
        name="attend_far",
    )(half.reshape(1), qkv, far_kv, far_kv, far_valid, w_proj, *state)


def attend(half, qkv, valid, far_kv, far_valid, w_proj, heads, tile=512):
    width = w_proj.shape[0]
    columns = w_proj.shape[1]
    queries = far_kv.shape[0]
    whole = lambda *shape: pl.BlockSpec(shape, lambda i, half: (0,) * len(shape))
    part = lambda c, w=width: pl.BlockSpec((queries, w), lambda i, half: (half[0], c))
    return pl.pallas_call(
        functools.partial(attend_kernel, heads, tile),
        out_shape=jax.ShapeDtypeStruct((queries, columns), jnp.bfloat16),
        grid_spec=pltpu.PrefetchScalarGridSpec(
            num_scalar_prefetch=1,
            grid=(1,),
            in_specs=[
                part(0), part(1), part(2), part(0, LANES),
                pl.BlockSpec((queries, width), lambda i, half: (0, 0)),
                pl.BlockSpec((queries, width), lambda i, half: (0, 1)),
                whole(queries, LANES),
                whole(width, columns),
            ],
            out_specs=whole(queries, columns),
            scratch_shapes=[pltpu.VMEM((2 * queries, width), jnp.bfloat16)]
            + [pltpu.VMEM((width // LANES, 2 * queries, 2 * LANES), jnp.bfloat16)]
            + [pltpu.VMEM((queries, width), jnp.float32)] * 2
            + [pltpu.VMEM((2, tile, 2 * queries), jnp.float32)],
        ),
        cost_estimate=pl.CostEstimate(
            flops=heads * queries * 2 * queries * width * 4,
            bytes_accessed=queries * columns * 10,
            transcendentals=heads * queries * 2 * queries,
        ),
        name="attend",
    )(half.reshape(1), qkv, qkv, qkv, valid, far_kv, far_kv, far_valid, w_proj)


def shards(points, ln_gain, ln_bias, w_qkv, b_qkv, w_proj, b_proj, counts, hilbert_pos):
    regions = lax.axis_size("region")
    heads_axis = lax.axis_size("head")
    r = lax.axis_index("region")
    h = lax.axis_index("head")
    rows, model_width = points.shape
    group_width = w_qkv.shape[2]
    heads = group_width // HD
    width = max(group_width, LANES)
    blocks = rows // BS
    total_blocks = blocks * regions
    slots = max(2, 2 * blocks // regions)
    half_rows = PATCH // 2
    half_blocks = half_rows // BS

    position = jnp.arange(blocks, dtype=jnp.int32)
    my_dest = lax.dynamic_slice_in_dim(hilbert_pos, r * blocks, blocks) // blocks
    earlier = (my_dest[:, None] == my_dest[None, :]) & (position[None, :] < position[:, None])
    my_slot = my_dest * slots + jnp.sum(earlier, axis=1, dtype=jnp.int32)
    pack_table = jnp.sum(
        jnp.where(
            my_slot[None, :] == jnp.arange(regions * slots, dtype=jnp.int32)[:, None],
            position[None, :], 0,
        ),
        axis=1, dtype=jnp.int32,
    )
    every = jnp.arange(total_blocks, dtype=jnp.int32)
    ext = (
        r * blocks - half_blocks + jnp.arange(blocks + 2 * half_blocks, dtype=jnp.int32)
        + total_blocks
    ) % total_blocks
    here = hilbert_pos[None, :] == ext[:, None]
    ext_counts = jnp.sum(jnp.where(here, counts[None, :], 0), axis=1, dtype=jnp.int32)
    origin = jnp.sum(
        jnp.where(here[half_blocks:half_blocks + blocks], every[None, :], 0),
        axis=1, dtype=jnp.int32,
    )
    same = (
        (every[None, :] < origin[:, None])
        & (every[None, :] // blocks == origin[:, None] // blocks)
        & (hilbert_pos[None, :] // blocks == r)
    )
    slot_table = origin // blocks * slots + jnp.sum(same, axis=1, dtype=jnp.int32)
    own_counts = ext_counts[half_blocks:half_blocks + blocks]
    valid_ext = (
        jnp.arange(BS, dtype=jnp.int32)[None, :, None] < ext_counts[:, None, None]
    )
    valid_ext = jnp.broadcast_to(valid_ext, (blocks + 2 * half_blocks, BS, LANES))
    valid_ext = valid_ext.reshape(-1, LANES).astype(jnp.bfloat16)

    packed = pack_blocks(points, ln_gain, ln_bias, h, pack_table, heads_axis)
    recv = exchange(packed, regions, heads_axis)

    pad = width - group_width
    weight = jnp.pad(w_qkv, ((0, 0), (0, 0), (0, pad))).reshape(model_width, 3 * width)
    bias = jnp.pad(b_qkv, ((0, 0), (0, pad))).reshape(3 * width)
    w_out = jnp.pad(w_proj, ((0, pad), (0, 0)))
    valid = valid_ext[half_rows:half_rows + rows]
    qkv = project(recv, slot_table, own_counts, valid, weight, bias)

    if heads_axis == 2:
        order = (1 - h, h)
        flat = lambda a, b: (a % regions) * 2 + b
        fars = []
        for turn in range(2):
            pairs = []
            for i in range(regions):
                for b in range(2):
                    upper = (1 - b if turn == 0 else b) == 1
                    pairs.append((flat(i + 1 if upper else i - 1, b), flat(i, b)))
            start = (1 - order[turn]) * half_rows
            piece = lax.dynamic_slice(qkv, (start, width), (half_rows, 2 * width))
            fars.append(lax.ppermute(piece, ("region", "head"), pairs))
        partials = []
        for turn in range(2):
            half = order[turn]
            far_valid = lax.dynamic_slice(
                valid_ext, (half * (rows + half_rows), 0), (half_rows, LANES)
            )
            if turn == 0:
                state = attend_near(half, qkv, valid, width, half_rows, heads)
                partials.append(
                    attend_far(half, qkv, fars[0], far_valid, w_out, state, heads)
                )
                arrived = lax.ppermute(partials[0], "head", [(0, 1), (1, 0)])
            else:
                partials.append(attend(half, qkv, valid, fars[1], far_valid, w_out, heads))
        summed_rows = partials[1].astype(jnp.float32) + arrived.astype(jnp.float32)
    else:
        up = [(i, (i + 1) % regions) for i in range(regions)]
        down = [(j, i) for i, j in up]
        kv = qkv[:, width:]
        before = lax.ppermute(kv[rows - half_rows:], "region", up)
        after = lax.ppermute(kv[:half_rows], "region", down)
        partials = [
            attend(jnp.int32(0), qkv, valid, before, valid_ext[:half_rows], w_out, heads),
            attend(jnp.int32(1), qkv, valid, after, valid_ext[rows + half_rows:], w_out, heads),
        ]
        summed_rows = lax.psum_scatter(
            jnp.concatenate(partials, axis=0), "head", scatter_dimension=0, tiled=True
        ).astype(jnp.float32)
    share = rows // heads_axis
    share_valid = lax.dynamic_slice(valid, (h * share, 0), (share, LANES))[:, :1] > 0
    return jnp.where(share_valid, summed_rows + b_proj, 0.0).astype(jnp.bfloat16)


def solution(mesh):
    return jax.shard_map(
        shards,
        mesh=mesh,
        in_specs=(
            P("region", None),
            P(),
            P(),
            P(None, None, "head"),
            P(None, "head"),
            P("head", None),
            P(),
            P(),
            P(),
        ),
        out_specs=P(("region", "head"), None),
        check_vma=False,
    )
```

profile of v0, /device:TPU:0, one launch (start us, length us, event | category | flops | bytes accessed | tf_op | source)
XLA Modules:
  0.0 106.3 jit_solution(519418231303341947)
XLA Ops:
  0.0 0.7 fusion.5
  0.7 0.8 broadcast_compare_fusion
  1.5 0.9 select_reduce_fusion
  2.4 0.1 fusion.2
  2.4 0.7 slice.17.count_ref
  3.1 0.8 and_select_fusion
  3.9 0.2 convert_reduce_fusion.1
  4.0 0.8 multiply_add_fusion
  4.8 0.6 select_reduce_fusion.2.pack_ref
  5.4 3.4 %pack.1.send = bf16[2048,256]{1,0:T(8,128)(2,1)} custom-call(s32[64]{0:T(128)} %select_reduce_fusion.2.pack_ref, s32[1]{0:T(128)} %bitcast.head_ref.half_ref, bf16[1024,512]{1,0:T(8,128)(2,1)} %x_ref.1, f32[1,512]{1,0:T(1,128)} %bitcast.11, f32[1,512]{1,0:T(1,128)} %bitcast.12), custom_call_target="tpu_custom_call" | custom-call | tf_op jit(solution)/shard_map/pack/pallas_call | solution.py:58
  8.8 41.6 %exchange.1.recv = bf16[2,2048,256]{2,1,0:T(8,128)(2,1)} custom-call(bf16[2048,256]{1,0:T(8,128)(2,1)} %pack.1.send), custom_call_target="tpu_custom_call" | custom-call | tf_op jit(solution)/shard_map/exchange/pallas_call | solution.py:172
  50.4 0.1 select_reduce_fusion.1
  50.6 0.2 convert_reduce_fusion
  50.8 0.5 multiply_add_fusion.1.slot_ref
  51.3 0.1 slice.15
  51.4 0.3 copy.13
  51.7 1.2 %copy.14.w_ref = bf16[512,768]{1,0:T(8,128)(2,1)} copy(bf16[512,768]{0,1:T(8,128)(2,1)S(1)} %bitcast.8) | data formatting | bytes 1572864 | tf_op jit(solution)/shard_map/reshape | solution.py:502
  52.8 0.6 copy.15
  53.4 0.9 broadcast_in_dim.86.valid_ref.on_ref
  54.3 4.8 %project.1.q_ref.kn_ref.vn_ref = bf16[1024,768]{1,0:T(8,128)(2,1)} custom-call(s32[32]{0:T(128)} %multiply_add_fusion.1.slot_ref, s32[32]{0:T(128)} %slice.17.count_ref, bf16[2,2048,256]{2,1,0:T(8,128)(2,1)} %exchange.1.recv, bf16[1024,128]{1,0:T(8,128)(2,1)} %broadcast_in_dim.86.valid_ref.on_ref, bf16[512,768]{1,0:T(8,128)(2,1)} %copy.14.w_ref, ...), custom_call_target="tpu_custom_call" | custom-call | tf_op jit(solution)/shard_map/project/pallas_call | solution.py:231
  59.1 1.3 %constant_dynamic-slice_fusion.1 = (bf16[512,512]{1,0:T(8,128)(2,1)S(1)}, bf16[512,512]{1,0:T(8,128)(2,1)S(1)}) fusion(bf16[1024,768]{1,0:T(8,128)(2,1)} %project.1.q_ref.kn_ref.vn_ref, s32[]{:T(128)S(6)} %select_n.83, s32[]{:T(128)S(6)} %select_n.75), kind=kLoop, calls=%fused_computation.43 | loop fusion | bytes 2097160 | tf_op jit(solution)/shard_map/dynamic_slice | solution.py:519
  60.4 7.2 %collective-permute-start.1 = (bf16[512,512]{1,0:T(8,128)(2,1)S(1)}, bf16[512,512]{1,0:T(8,128)(2,1)S(1)}, u32[]{:S(2)}, u32[]{:S(2)}) collective-permute-start(bf16[512,512]{1,0:T(8,128)(2,1)S(1)} %get-tuple-element.12), channel_id=1, source_target_pairs={{2,0},{31,1},{4,2},{1,3},{6,4},{3,5},{8,6},{5,7},{10,8},{7,9},{12,... | collective-permute-start | bytes 1572872 | tf_op jit(solution)/shard_map/ppermute | solution.py:520
  67.6 8.5 %attend_near.1 = (f32[512,256]{1,0:T(8,128)}, f32[512,256]{1,0:T(8,128)}, f32[512,128]{1,0:T(8,128)}) custom-call(s32[1]{0:T(128)} %bitcast.4.half_ref, bf16[1024,768]{1,0:T(8,128)(2,1)} %project.1.q_ref.kn_ref.vn_ref, bf16[1024,768]{1,0:T(8,128)(2,1)} %project.1.q_ref.kn_ref.vn_ref, bf16[1024,768]{1,0:T(8,128)(2,1)} %project.1.q_ref.kn_ref.vn_ref, ...), custom_call_target="tpu_custom_call" | custom-call | flops 4294967296 | bytes 2621440 | tf_op jit(solution)/shard_map/attend_near/pallas_call | solution.py:362
  76.1 0.1 dynamic-slice_compare_fusion
  76.2 0.1 convert_element_type.25
  76.3 0.1 fusion.11
  76.4 0.8 broadcast_in_dim.88.of_ref
  77.2 9.5 %attend_far.1 = bf16[512,512]{1,0:T(8,128)(2,1)} custom-call(s32[1]{0:T(128)} %bitcast.4.half_ref, bf16[1024,768]{1,0:T(8,128)(2,1)} %project.1.q_ref.kn_ref.vn_ref, bf16[512,512]{1,0:T(8,128)(2,1)} %copy-done.4, bf16[512,512]{1,0:T(8,128)(2,1)} %copy-done.4, bf16[512,128]{1,0:T(8,128)(2,1)} %broadcast_in_dim.88.of_ref, bf16[256,512]{1,0:T(8,128)(2,1)} %w_ref.3, ...), custom_call_target="tpu_custom_call" | custom-call | flops 4294967296 | bytes 2621440 | tf_op jit(solution)/shard_map/attend_far/pallas_call | solution.py:389
  86.7 2.8 %collective-permute-start.2 = (bf16[512,512]{1,0:T(8,128)(2,1)}, bf16[512,512]{1,0:T(8,128)(2,1)S(1)}, u32[]{:S(2)}, u32[]{:S(2)}) collective-permute-start(bf16[512,512]{1,0:T(8,128)(2,1)} %attend_far.1), channel_id=1, source_target_pairs={{0,1},{1,0},{2,3},{3,2},{4,5},{5,4},{6,7},{7,6},{8,9},{9,8},{10,11... | collective-permute-start | bytes 1572872 | tf_op jit(solution)/shard_map/ppermute | solution.py:532
  89.5 0.8 broadcast_in_dim.87.of_ref
  90.3 13.9 %attend.1 = bf16[512,512]{1,0:T(8,128)(2,1)} custom-call(s32[1]{0:T(128)} %bitcast.head_ref.half_ref, bf16[1024,768]{1,0:T(8,128)(2,1)} %project.1.q_ref.kn_ref.vn_ref, bf16[1024,768]{1,0:T(8,128)(2,1)} %project.1.q_ref.kn_ref.vn_ref, bf16[1024,768]{1,0:T(8,128)(2,1)} %project.1.q_ref.kn_ref.vn_ref, bf16[1024,128]{1,0:T(8,128)(2,1)} %broadcast_in_dim.86.valid_ref.on_ref, ...), custom_call_target="tpu_custom_call" | custom-call | flops 8589934592 | bytes 2621440 | tf_op jit(solution)/shard_map/attend/pallas_call | solution.py:420
  104.2 2.1 %select_convert_fusion = bf16[512,512]{1,0:T(8,128)(2,1)} fusion(bf16[512,512]{1,0:T(8,128)(2,1)S(1)} %collective-permute-done.2, bf16[512,512]{1,0:T(8,128)(2,1)} %attend.1, f32[512]{0:T(512)S(1)} %copy-done.2, pred[512]{0:T(512)(128)(4,1)S(1)} %dynamic-slice_compare_fusion), kind=kLoop, calls=%fused_computation | loop fusion | flops 1572864 | bytes 1575424 | tf_op jit(solution)/shard_map/convert_element_type | solution.py:551
  (18 shorter events, 0.1 us)
Async XLA Ops:
  8.8 42.6 %copy-start = (bf16[512,3,256]{2,0,1:T(8,128)(2,1)S(1)}, bf16[512,3,256]{2,0,1:T(8,128)(2,1)}, u32[]{:S(2)}) copy-start(bf16[512,3,256]{2,0,1:T(8,128)(2,1)} %param.12) | copy-start | bytes 2359300
  51.4 1.5 %copy-start.1 = (f32[3,256]{1,0:T(4,128)S(1)}, f32[3,256]{1,0:T(4,128)}, u32[]{:S(2)}) copy-start(f32[3,256]{1,0:T(4,128)} %param.13) | copy-start | bytes 9220
  60.4 29.1 %collective-permute-start = (bf16[512,512]{1,0:T(8,128)(2,1)S(1)}, bf16[512,512]{1,0:T(8,128)(2,1)S(1)}, u32[]{:S(2)}, u32[]{:S(2)}) collective-permute-start(bf16[512,512]{1,0:T(8,128)(2,1)S(1)} %get-tuple-element.11), channel_id=1, source_target_pairs={{30,0},{3,1},{0,2},{5,3},{2,4},{7,5},{4,6},{9,7},{6,8},{11,9},{8,1... | collective-permute-start | bytes 1572872 | tf_op jit(solution)/shard_map/ppermute | solution.py:520
  60.4 15.9 %collective-permute-start.1 = (bf16[512,512]{1,0:T(8,128)(2,1)S(1)}, bf16[512,512]{1,0:T(8,128)(2,1)S(1)}, u32[]{:S(2)}, u32[]{:S(2)}) collective-permute-start(bf16[512,512]{1,0:T(8,128)(2,1)S(1)} %get-tuple-element.12), channel_id=1, source_target_pairs={{2,0},{31,1},{4,2},{1,3},{6,4},{3,5},{8,6},{5,7},{10,8},{7,9},{12,... | collective-permute-start | bytes 1572872 | tf_op jit(solution)/shard_map/ppermute | solution.py:520
  76.4 0.8 copy-start.4
  86.7 17.5 %collective-permute-start.2 = (bf16[512,512]{1,0:T(8,128)(2,1)}, bf16[512,512]{1,0:T(8,128)(2,1)S(1)}, u32[]{:S(2)}, u32[]{:S(2)}) collective-permute-start(bf16[512,512]{1,0:T(8,128)(2,1)} %attend_far.1), channel_id=1, source_target_pairs={{0,1},{1,0},{2,3},{3,2},{4,5},{5,4},{6,7},{7,6},{8,9},{9,8},{10,11... | collective-permute-start | bytes 1572872 | tf_op jit(solution)/shard_map/ppermute | solution.py:532
  89.5 0.8 copy-start.3
  90.3 13.9 %copy-start.2 = (f32[512]{0:T(512)S(1)}, f32[512]{0:T(512)}, u32[]{:S(2)}) copy-start(f32[512]{0:T(512)} %param.15) | copy-start | bytes 6148
where the time goes:
time: 107 us; the launch traced here: 106 us
  Pallas kernels  81.7 us (76%)
  starting transfers between devices  10 us (9%)
  other arithmetic  7.72 us (7%)
  local copies, waits for them, and re-layouts  6.75 us (6%)
    pallas_call x1, Pallas kernels, exchange(): pl.pallas_call(functools.partial(exchange_kernel, regions, heads_axis, ro...  41.6 us
    pallas_call x1, Pallas kernels, attend(): pl.pallas_call(functools.partial(attend_kernel, heads, tile), out_shape=j...  13.9 us
    pallas_call x1, Pallas kernels, attend_far(): pl.pallas_call(functools.partial(far_kernel, heads, tile), out_shape=jax....  9.52 us
    pallas_call x1, Pallas kernels, attend_near(): pl.pallas_call(functools.partial(near_kernel, heads, tile), out_shape=[ja...  8.53 us
    ppermute x2, starting transfers between devices, shards(): fars.append(lax.ppermute(piece, ('region', 'head'), pairs))  7.22 us
    pallas_call x1, Pallas kernels, project(): pl.pallas_call(functools.partial(project_kernel, blocks, tile), out_shape...  4.76 us
    pallas_call x1, Pallas kernels, pack_blocks(): pl.pallas_call(functools.partial(pack_kernel, total, parts, tile), out_sh...  3.39 us
    ppermute x1, starting transfers between devices, shards(): arrived = lax.ppermute(partials[0], 'head', [(0, 1), (1, 0)])  2.79 us
  transfers between devices with their start and end apart: 3, of which 0 were waited for; matrix products, arithmetic and copies ran while one was open for 2% of the time, Pallas kernels for 30%

commit v1 on v0

--- a/solution.py
+++ b/solution.py
@@ -443,6 +443,278 @@
         ),
         name="attend",
     )(half.reshape(1), qkv, qkv, qkv, valid, far_kv, far_kv, far_valid, w_proj)
+
+
+def gather_kernel(slots, pos_ref, x_ref, out_ref, taken):
+    rows, depth = x_ref.shape
+    parts, _, width = out_ref.shape
+    blocks = rows // BS
+    first = lax.axis_index("region") * blocks
+    for d in range(taken.shape[0]):
+        taken[d] = 0
+
+    def place(i, carry):
+        target = lax.div(pos_ref[first + i], blocks)
+        used = taken[target]
+        taken[target] = used + 1
+        into = pl.ds(pl.multiple_of((target * slots + used) * BS, BS), BS)
+        source = pl.ds(pl.multiple_of(i * BS, BS), BS)
+        for part in range(parts):
+            out_ref[part, into, :] = x_ref[source, part * width:(part + 1) * width]
+        return carry
+
+    lax.fori_loop(0, blocks, place, 0, unroll=4)
+
+
+def gather_blocks(points, hilbert_pos, regions, slots, parts):
+    rows, depth = points.shape
+    vmem = pl.BlockSpec(memory_space=pltpu.VMEM)
+    return pl.pallas_call(
+        functools.partial(gather_kernel, slots),
+        out_shape=jax.ShapeDtypeStruct(
+            (parts, regions * slots * BS, depth // parts), jnp.bfloat16
+        ),
+        in_specs=[pl.BlockSpec(memory_space=pltpu.SMEM), vmem],
+        out_specs=vmem,
+        scratch_shapes=[pltpu.SMEM((regions,), jnp.int32)],
+        name="gather_blocks",
+    )(hilbert_pos, points)
+
+
+def swap_kernel(
+    regions, near,
+    send, gain_ref, bias_ref, w_ref, b_ref, made,
+    recv, send_sem, recv_sem, relay_sem,
+):
+    r = lax.axis_index("region")
+    h = lax.axis_index("head")
+    other = 1 - h
+    chunk = recv.shape[1] // regions
+    piece = recv.shape[2]
+    width = w_ref.shape[2]
+    seat = lax.rem(r, near)
+    base = r - seat
+    far = regions - near
+    lag = 2
+
+    barrier = pltpu.get_barrier_semaphore()
+
+    def greet(d, carry):
+        pl.semaphore_signal(
+            barrier, inc=1, device_id={"region": lax.rem(r + d, regions)}, device_id_type=MESH
+        )
+        return carry
+
+    lax.fori_loop(1, regions, greet, 0)
+    pl.semaphore_signal(barrier, inc=1, device_id={"head": other}, device_id_type=MESH)
+    pl.semaphore_wait(barrier, regions)
+
+    def rows(s):
+        return pl.ds(pl.multiple_of(s * chunk, chunk), chunk)
+
+    def to_region(t, part):
+        return pltpu.make_async_remote_copy(
+            src_ref=send.at[part, rows(t)],
+            dst_ref=recv.at[part, rows(r)],
+            send_sem=send_sem.at[part, t],
+            recv_sem=recv_sem.at[part, r],
+            device_id={"region": t},
+            device_id_type=MESH,
+        )
+
+    def arrival(s, part):
+        return pltpu.make_async_remote_copy(
+            src_ref=send.at[part, rows(s)],
+            dst_ref=recv.at[part, rows(s)],
+            send_sem=send_sem.at[part, s],
+            recv_sem=recv_sem.at[part, s],
+            device_id={"head": other},
+            device_id_type=MESH,
+        )
+
+    def relay(s):
+        return pltpu.make_async_remote_copy(
+            src_ref=recv.at[h, rows(s)],
+            dst_ref=recv.at[h, rows(s)],
+            send_sem=relay_sem.at[s],
+            recv_sem=recv_sem.at[h, s],
+            device_id={"head": other},
+            device_id_type=MESH,
+        )
+
+    def keep(part):
+        return pltpu.make_async_copy(
+            send.at[part, rows(r)], recv.at[part, rows(r)], recv_sem.at[part, r]
+        )
+
+    def near_target(j):
+        return base + lax.rem(seat + j, near)
+
+    def far_target(j):
+        group = lax.div(j, near)
+        return lax.rem(base + near * (group + 1), regions) + lax.rem(seat + lax.rem(j, near), near)
+
+    def near_source(j):
+        return base + lax.rem(seat + near - j, near)
+
+    def far_source(j):
+        group = lax.div(j, near)
+        return lax.rem(base + regions - near * (group + 1), regions) + lax.rem(
+            seat + near - lax.rem(j, near), near
+        )
+
+    keep(0).start()
+    keep(1).start()
+
+    def push_near(j, carry):
+        t = near_target(j)
+        to_region(t, 0).start()
+        to_region(t, 1).start()
+        return carry
+
+    def push_far(j, carry):
+        to_region(far_target(j), h).start()
+        return carry
+
+    lax.fori_loop(1, near, push_near, 0)
+    lax.fori_loop(0, far, push_far, 0)
+
+    def project(s):
+        part = rows(s)
+        left = recv[0, part, :].astype(jnp.float32)
+        right = recv[1, part, :].astype(jnp.float32)
+        depth = 2 * piece
+        mean = (
+            jnp.sum(left, axis=-1, keepdims=True) + jnp.sum(right, axis=-1, keepdims=True)
+        ) * (1.0 / depth)
+        left = left - mean
+        right = right - mean
+        row_var = (
+            jnp.sum(left * left, axis=-1, keepdims=True)
+            + jnp.sum(right * right, axis=-1, keepdims=True)
+        ) * (1.0 / depth)
+        scale = lax.rsqrt(row_var + epsilon)
+        left = (left * scale * gain_ref[:, :piece] + bias_ref[:, :piece]).astype(jnp.bfloat16)
+        right = (right * scale * gain_ref[:, piece:] + bias_ref[:, piece:]).astype(jnp.bfloat16)
+        for c in range(3):
+            summed = jnp.dot(left, w_ref[c, :piece, :], preferred_element_type=jnp.float32)
+            summed = summed + jnp.dot(
+                right, w_ref[c, piece:, :], preferred_element_type=jnp.float32
+            )
+            summed = summed + b_ref[c:c + 1, :]
+            if c == 0:
+                summed = summed * HD ** (-0.5)
+            made[part, c * width:(c + 1) * width] = summed.astype(jnp.bfloat16)
+
+    ahead = near - lag
+
+    def forward(j):
+        s = far_source(j)
+        arrival(s, h).wait_recv()
+        relay(s).start()
+
+    def close(i, carry):
+        @pl.when(i >= lag)
+        def _():
+            forward(i - lag)
+
+        s = near_source(i)
+        arrival(s, 0).wait_recv()
+        arrival(s, 1).wait_recv()
+        project(s)
+        return carry
+
+    def distant(j, carry):
+        @pl.when(j < far - ahead)
+        def _():
+            forward(j + ahead)
+
+        s = far_source(j)
+        arrival(s, other).wait_recv()
+        project(s)
+        return carry
+
+    lax.fori_loop(0, near, close, 0)
+    lax.fori_loop(0, far, distant, 0)
+
+    def drain_near(j, carry):
+        t = near_target(j)
+        to_region(t, 0).wait_send()
+        to_region(t, 1).wait_send()
+        return carry
+
+    def drain_far(j, carry):
+        to_region(far_target(j), h).wait_send()
+        relay(far_source(j)).wait_send()
+        return carry
+
+    lax.fori_loop(1, near, drain_near, 0)
+    lax.fori_loop(0, far, drain_far, 0)
+
+
+def swap(send, ln_gain, ln_bias, weight, bias, regions):
+    parts, rows, piece = send.shape
+    width = weight.shape[2]
+    vmem = pl.BlockSpec(memory_space=pltpu.VMEM)
+    return pl.pallas_call(
+        functools.partial(swap_kernel, regions, regions // 4),
+        out_shape=jax.ShapeDtypeStruct((rows, 3 * width), jnp.bfloat16),
+        in_specs=[pl.BlockSpec(memory_space=pl.ANY), vmem, vmem, vmem, vmem],
+        out_specs=vmem,
+        scratch_shapes=[
+            pltpu.VMEM((parts, rows, piece), jnp.bfloat16),
+            pltpu.SemaphoreType.DMA((parts, regions)),
+            pltpu.SemaphoreType.DMA((parts, regions)),
+            pltpu.SemaphoreType.DMA((regions,)),
+        ],
+        compiler_params=pltpu.CompilerParams(collective_id=1, has_side_effects=True),
+        name="swap",
+    )(send, ln_gain.reshape(1, -1), ln_bias.reshape(1, -1), weight, bias)
+
+
+def unpack_kernel(slot_ref, count_ref, made, out_ref, sems):
+    blocks = slot_ref.shape[0]
+    width = out_ref.shape[1] // 3
+
+    def fetch(t):
+        return pltpu.make_async_copy(
+            made.at[pl.ds(pl.multiple_of(slot_ref[t] * BS, BS), BS)],
+            out_ref.at[pl.ds(pl.multiple_of(t * BS, BS), BS)],
+            sems.at[t],
+        )
+
+    def begin(t, carry):
+        fetch(t).start()
+        return carry
+
+    lax.fori_loop(0, blocks, begin, 0)
+    row_index = lax.broadcasted_iota(jnp.int32, (BS, width), 0)
+
+    def mask(t, carry):
+        fetch(t).wait()
+        into = pl.ds(pl.multiple_of(t * BS, BS), BS)
+        live = row_index < count_ref[t]
+        keys = out_ref[into, width:2 * width].astype(jnp.float32)
+        out_ref[into, width:2 * width] = jnp.where(live, keys, keys[0:1, :]).astype(jnp.bfloat16)
+        vals = out_ref[into, 2 * width:].astype(jnp.float32)
+        out_ref[into, 2 * width:] = jnp.where(live, vals, 0.0).astype(jnp.bfloat16)
+        return carry
+
+    lax.fori_loop(0, blocks, mask, 0, unroll=4)
+
+
+def unpack_blocks(made, slot_table, own_counts):
+    blocks = slot_table.shape[0]
+    vmem = pl.BlockSpec(memory_space=pltpu.VMEM)
+    smem = pl.BlockSpec(memory_space=pltpu.SMEM)
+    return pl.pallas_call(
+        unpack_kernel,
+        out_shape=jax.ShapeDtypeStruct((blocks * BS, made.shape[1]), jnp.bfloat16),
+        in_specs=[smem, smem, pl.BlockSpec(memory_space=pl.ANY)],
+        out_specs=vmem,
+        scratch_shapes=[pltpu.SemaphoreType.DMA((blocks,))],
+        name="unpack_blocks",
+    )(slot_table, own_counts, made)
 
 
 def shards(points, ln_gain, ln_bias, w_qkv, b_qkv, w_proj, b_proj, counts, hilbert_pos):
@@ -495,15 +767,21 @@
     valid_ext = jnp.broadcast_to(valid_ext, (blocks + 2 * half_blocks, BS, LANES))
     valid_ext = valid_ext.reshape(-1, LANES).astype(jnp.bfloat16)
 
-    packed = pack_blocks(points, ln_gain, ln_bias, h, pack_table, heads_axis)
-    recv = exchange(packed, regions, heads_axis)
-
     pad = width - group_width
-    weight = jnp.pad(w_qkv, ((0, 0), (0, 0), (0, pad))).reshape(model_width, 3 * width)
-    bias = jnp.pad(b_qkv, ((0, 0), (0, pad))).reshape(3 * width)
+    valid = valid_ext[half_rows:half_rows + rows]
     w_out = jnp.pad(w_proj, ((0, pad), (0, 0)))
-    valid = valid_ext[half_rows:half_rows + rows]
-    qkv = project(recv, slot_table, own_counts, valid, weight, bias)
+    if heads_axis == 2:
+        send = gather_blocks(points, hilbert_pos, regions, slots, heads_axis)
+        made = swap(
+            send, ln_gain, ln_bias, jnp.transpose(w_qkv, (1, 0, 2)), b_qkv, regions
+        )
+        qkv = unpack_blocks(made, slot_table, own_counts)
+    else:
+        packed = pack_blocks(points, ln_gain, ln_bias, h, pack_table, heads_axis)
+        recv = exchange(packed, regions, heads_axis)
+        weight = jnp.pad(w_qkv, ((0, 0), (0, 0), (0, pad))).reshape(model_width, 3 * width)
+        bias = jnp.pad(b_qkv, ((0, 0), (0, pad))).reshape(3 * width)
+        qkv = project(recv, slot_table, own_counts, valid, weight, bias)
 
     if heads_axis == 2:
         order = (1 - h, h)

time: 107 us -> 97 us (0.907)
  Pallas kernels: 81.7 us -> 76.8 us
  other arithmetic: 7.72 us -> 5.41 us
  local copies, waits for them, and re-layouts: 6.75 us -> 4.71 us
    pallas_call x3, Pallas kernels: 49.8 us -> 44.9 us  [the longest x1 38.5 us: swap(): pl.pallas_call(functools.partial(swap_kernel, regions, regions // 4), out...]
    ppermute x1, starting transfers between devices: 2.79 us -> 1.33 us  [shards(): arrived = lax.ppermute(partials[0], 'head', [(0, 1), (1, 0)])]
    reshape x1 -> x0, local copies, waits for them, and re-layouts: 1.16 us -> none  [shards(): jnp.pad(w_qkv, ((0, 0), (0, 0), (0, pad))).reshape(model_width, 3 * width)]
  transfers between devices with their start and end apart: 3 -> 3, of which waited for: 0 -> 0; matrix products, arithmetic and copies ran while one was open for 2% -> 3% of each run, Pallas kernels for 30% -> 33%
where the time goes in v1:
time: 97 us; the launch traced here: 96.5 us
  Pallas kernels  76.8 us (79%)
  starting transfers between devices  9.53 us (10%)
  other arithmetic  5.41 us (6%)
  local copies, waits for them, and re-layouts  4.71 us (5%)
    pallas_call x1, Pallas kernels, swap(): pl.pallas_call(functools.partial(swap_kernel, regions, regions // 4), out...  38.5 us
    pallas_call x1, Pallas kernels, attend(): pl.pallas_call(functools.partial(attend_kernel, heads, tile), out_shape=j...  13.9 us
    pallas_call x1, Pallas kernels, attend_far(): pl.pallas_call(functools.partial(far_kernel, heads, tile), out_shape=jax....  9.51 us
    pallas_call x1, Pallas kernels, attend_near(): pl.pallas_call(functools.partial(near_kernel, heads, tile), out_shape=[ja...  8.53 us
    ppermute x2, starting transfers between devices, shards(): fars.append(lax.ppermute(piece, ('region', 'head'), pairs))  8.2 us
    pallas_call x1, Pallas kernels, unpack_blocks(): pl.pallas_call(unpack_kernel, out_shape=jax.ShapeDtypeStruct((blocks * BS...  3.53 us
    pallas_call x1, Pallas kernels, gather_blocks(): pl.pallas_call(functools.partial(gather_kernel, slots), out_shape=jax.Sha...  2.83 us
    broadcast_in_dim x3, local copies, waits for them, and re-layouts, shards(): jnp.broadcast_to(valid_ext, (blocks + 2 * half_blocks, BS, LANES))  2.58 us
  transfers between devices with their start and end apart: 3, of which 0 were waited for; matrix products, arithmetic and copies ran while one was open for 3% of the time, Pallas kernels for 33%

profile of v1, /device:TPU:0, one launch (start us, length us, event | category | flops | bytes accessed | tf_op | source)
XLA Modules:
  0.0 96.5 jit_solution(4874968446910259141)
XLA Ops:
  0.0 0.7 fusion.4
  0.7 0.8 broadcast_compare_fusion
  1.5 0.1 select_reduce_fusion.1
  1.6 0.2 convert_reduce_fusion
  1.8 0.5 multiply_add_fusion.slot_ref
  2.3 0.9 select_reduce_fusion
  3.2 0.6 slice.17.count_ref
  3.8 2.8 %gather_blocks.1.send = bf16[2,2048,256]{2,1,0:T(8,128)(2,1)} custom-call(s32[512]{0:T(512)} %pos_ref.1, bf16[1024,512]{1,0:T(8,128)(2,1)} %x_ref.1), custom_call_target="tpu_custom_call" | custom-call | tf_op jit(solution)/shard_map/gather_blocks/pallas_call | solution.py:472
  6.6 38.5 %swap.1.made = bf16[2048,768]{1,0:T(8,128)(2,1)} custom-call(bf16[2,2048,256]{2,1,0:T(8,128)(2,1)} %gather_blocks.1.send, f32[1,512]{1,0:T(1,128)} %bitcast.6, f32[1,512]{1,0:T(1,128)} %bitcast.7, bf16[3,512,256]{2,1,0:T(8,128)(2,1)} %bitcast.5, f32[3,256]{1,0:T(4,128)} %b_ref.1), custom_call_target="tpu_custom_call" | custom-call | tf_op jit(solution)/shard_map/swap/pallas_call | solution.py:659
  45.2 3.5 %unpack_blocks.1.q_ref.kn_ref.vn_ref = bf16[1024,768]{1,0:T(8,128)(2,1)} custom-call(s32[32]{0:T(128)} %multiply_add_fusion.slot_ref, s32[32]{0:T(128)} %slice.17.count_ref, bf16[2048,768]{1,0:T(8,128)(2,1)} %swap.1.made), custom_call_target="tpu_custom_call" | custom-call | tf_op jit(solution)/shard_map/unpack_blocks/pallas_call | solution.py:710
  48.7 1.3 %constant_dynamic-slice_fusion.1 = (bf16[512,512]{1,0:T(8,128)(2,1)S(1)}, bf16[512,512]{1,0:T(8,128)(2,1)S(1)}) fusion(bf16[1024,768]{1,0:T(8,128)(2,1)} %unpack_blocks.1.q_ref.kn_ref.vn_ref, s32[]{:T(128)S(6)} %select_n.70, s32[]{:T(128)S(6)} %select_n.65), kind=kLoop, calls=%fused_computation.34 | loop fusion | bytes 2097160 | tf_op jit(solution)/shard_map/dynamic_slice | solution.py:797
  50.0 0.1 collective-permute-start
  50.0 8.1 %collective-permute-start.1 = (bf16[512,512]{1,0:T(8,128)(2,1)S(1)}, bf16[512,512]{1,0:T(8,128)(2,1)S(1)}, u32[]{:S(2)}, u32[]{:S(2)}) collective-permute-start(bf16[512,512]{1,0:T(8,128)(2,1)S(1)} %get-tuple-element.12), channel_id=1, source_target_pairs={{2,0},{31,1},{4,2},{1,3},{6,4},{3,5},{8,6},{5,7},{10,8},{7,9},{12,... | collective-permute-start | bytes 1572872 | tf_op jit(solution)/shard_map/ppermute | solution.py:798
  58.2 0.1 fusion.2
  58.3 0.1 slice.15
  58.4 0.9 broadcast_in_dim.65.on_ref
  59.3 8.5 %attend_near.1 = (f32[512,256]{1,0:T(8,128)}, f32[512,256]{1,0:T(8,128)}, f32[512,128]{1,0:T(8,128)}) custom-call(s32[1]{0:T(128)} %bitcast.4.half_ref, bf16[1024,768]{1,0:T(8,128)(2,1)} %unpack_blocks.1.q_ref.kn_ref.vn_ref, bf16[1024,768]{1,0:T(8,128)(2,1)} %unpack_blocks.1.q_ref.kn_ref.vn_ref, bf16[1024,768]{1,0:T(8,128)(2,1)} %unpack_blocks.1.q_ref.kn_ref.vn_ref, ...), custom_call_target="tpu_custom_call" | custom-call | flops 4294967296 | bytes 2621440 | tf_op jit(solution)/shard_map/attend_near/pallas_call | solution.py:362
  67.8 0.1 dynamic-slice_compare_fusion
  67.9 0.1 convert_element_type.21
  68.0 0.1 fusion.10
  68.0 0.0 collective-permute-done.1.kf_ref.vf_ref
  68.0 0.8 broadcast_in_dim.67.of_ref
  68.9 0.0 copy-done.2
  68.9 9.5 %attend_far.1 = bf16[512,512]{1,0:T(8,128)(2,1)} custom-call(s32[1]{0:T(128)} %bitcast.4.half_ref, bf16[1024,768]{1,0:T(8,128)(2,1)} %unpack_blocks.1.q_ref.kn_ref.vn_ref, bf16[512,512]{1,0:T(8,128)(2,1)} %copy-done.2, bf16[512,512]{1,0:T(8,128)(2,1)} %copy-done.2, bf16[512,128]{1,0:T(8,128)(2,1)} %broadcast_in_dim.67.of_ref, bf16[256,512]{1,0:T(8,128)(2,1)} %w_ref.3, ...), custom_call_target="tpu_custom_call" | custom-call | flops 4294967296 | bytes 2621440 | tf_op jit(solution)/shard_map/attend_far/pallas_call | solution.py:389
  78.4 1.3 %collective-permute-start.2 = (bf16[512,512]{1,0:T(8,128)(2,1)}, bf16[512,512]{1,0:T(8,128)(2,1)S(1)}, u32[]{:S(2)}, u32[]{:S(2)}) collective-permute-start(bf16[512,512]{1,0:T(8,128)(2,1)} %attend_far.1), channel_id=1, source_target_pairs={{0,1},{1,0},{2,3},{3,2},{4,5},{5,4},{6,7},{7,6},{8,9},{9,8},{10,11... | collective-permute-start | bytes 1572872 | tf_op jit(solution)/shard_map/ppermute | solution.py:810
  79.7 0.0 collective-permute-done.kf_ref.vf_ref
  79.7 0.8 broadcast_in_dim.66.of_ref
  80.6 0.0 copy-done.1
  80.6 13.9 %attend.1 = bf16[512,512]{1,0:T(8,128)(2,1)} custom-call(s32[1]{0:T(128)} %bitcast.half_ref, bf16[1024,768]{1,0:T(8,128)(2,1)} %unpack_blocks.1.q_ref.kn_ref.vn_ref, bf16[1024,768]{1,0:T(8,128)(2,1)} %unpack_blocks.1.q_ref.kn_ref.vn_ref, bf16[1024,768]{1,0:T(8,128)(2,1)} %unpack_blocks.1.q_ref.kn_ref.vn_ref, bf16[1024,128]{1,0:T(8,128)(2,1)} %broadcast_in_dim.65.on_ref, ...), custom_call_target="tpu_custom_call" | custom-call | flops 8589934592 | bytes 2621440 | tf_op jit(solution)/shard_map/attend/pallas_call | solution.py:420
  94.4 0.0 collective-permute-done.2
  94.4 0.0 copy-done
  94.4 2.1 %select_convert_fusion = bf16[512,512]{1,0:T(8,128)(2,1)} fusion(bf16[512,512]{1,0:T(8,128)(2,1)S(1)} %collective-permute-done.2, bf16[512,512]{1,0:T(8,128)(2,1)} %attend.1, f32[512]{0:T(512)S(1)} %copy-done, pred[512]{0:T(512)(128)(4,1)S(1)} %dynamic-slice_compare_fusion), kind=kLoop, calls=%fused_computation | loop fusion | flops 1572864 | bytes 1575424 | tf_op jit(solution)/shard_map/convert_element_type | solution.py:829
  (7 shorter events, 0.0 us)
Async XLA Ops:
  50.0 29.8 %collective-permute-start = (bf16[512,512]{1,0:T(8,128)(2,1)S(1)}, bf16[512,512]{1,0:T(8,128)(2,1)S(1)}, u32[]{:S(2)}, u32[]{:S(2)}) collective-permute-start(bf16[512,512]{1,0:T(8,128)(2,1)S(1)} %get-tuple-element.11), channel_id=1, source_target_pairs={{30,0},{3,1},{0,2},{5,3},{2,4},{7,5},{4,6},{9,7},{6,8},{11,9},{8,1... | collective-permute-start | bytes 1572872 | tf_op jit(solution)/shard_map/ppermute | solution.py:798
  50.0 18.0 %collective-permute-start.1 = (bf16[512,512]{1,0:T(8,128)(2,1)S(1)}, bf16[512,512]{1,0:T(8,128)(2,1)S(1)}, u32[]{:S(2)}, u32[]{:S(2)}) collective-permute-start(bf16[512,512]{1,0:T(8,128)(2,1)S(1)} %get-tuple-element.12), channel_id=1, source_target_pairs={{2,0},{31,1},{4,2},{1,3},{6,4},{3,5},{8,6},{5,7},{10,8},{7,9},{12,... | collective-permute-start | bytes 1572872 | tf_op jit(solution)/shard_map/ppermute | solution.py:798
  68.0 0.8 copy-start.2
  78.4 16.0 %collective-permute-start.2 = (bf16[512,512]{1,0:T(8,128)(2,1)}, bf16[512,512]{1,0:T(8,128)(2,1)S(1)}, u32[]{:S(2)}, u32[]{:S(2)}) collective-permute-start(bf16[512,512]{1,0:T(8,128)(2,1)} %attend_far.1), channel_id=1, source_target_pairs={{0,1},{1,0},{2,3},{3,2},{4,5},{5,4},{6,7},{7,6},{8,9},{9,8},{10,11... | collective-permute-start | bytes 1572872 | tf_op jit(solution)/shard_map/ppermute | solution.py:810
  79.7 0.8 copy-start.1
  80.6 13.9 %copy-start = (f32[512]{0:T(512)S(1)}, f32[512]{0:T(512)}, u32[]{:S(2)}) copy-start(f32[512]{0:T(512)} %param.15) | copy-start | bytes 6148

commit v2 on v1

--- a/solution.py
+++ b/solution.py
@@ -13,6 +13,7 @@
 LANES = 128
 
 epsilon = 1e-05
+LOG2E = 1.4426950408889634
 MESH = pl.DeviceIdType.MESH
 
 
@@ -305,27 +306,6 @@
         vals[c, first:first + count, LANES:] = on_ref[...]
 
 
-def near_kernel(
-    heads, tile, half_ref, q_ref, kn_ref, vn_ref, on_ref, acc, den, peaks, vals, ahead
-):
-    fill_values(vals, vn_ref, on_ref, 0)
-    acc[...] = jnp.zeros_like(acc)
-    den[...] = jnp.ones_like(den)
-    peaks[...] = jnp.zeros_like(peaks)
-    over_heads(heads, tile, q_ref, kn_ref, vals, acc, den, ahead, peaks_out=peaks)
-
-
-def far_kernel(
-    heads, tile, half_ref, q_ref, kf_ref, vf_ref, of_ref, w_ref, acc0, den0, peaks, out_ref,
-    vals, acc, den, ahead,
-):
-    fill_values(vals, vf_ref, of_ref, 0)
-    acc[...] = acc0[...]
-    den[...] = den0[...]
-    over_heads(heads, tile, q_ref, kf_ref, vals, acc, den, ahead, peaks_in=peaks)
-    finish_heads(acc, den, w_ref, out_ref)
-
-
 def attend_kernel(
     heads, tile,
     half_ref, q_ref, kn_ref, vn_ref, on_ref, kf_ref, vf_ref, of_ref, w_ref, out_ref,
@@ -356,59 +336,6 @@
         bytes_accessed=queries * width * 20,
         transcendentals=heads * queries * keys,
     )
-
-
-def attend_near(half, qkv, valid, width, queries, heads, tile=512):
-    return pl.pallas_call(
-        functools.partial(near_kernel, heads, tile),
-        out_shape=[
-            jax.ShapeDtypeStruct((queries, width), jnp.float32),
-            jax.ShapeDtypeStruct((queries, width), jnp.float32),
-            jax.ShapeDtypeStruct((queries, LANES), jnp.float32),
-        ],
-        grid_spec=pltpu.PrefetchScalarGridSpec(
-            num_scalar_prefetch=1,
-            grid=(1,),
-            in_specs=[half_block(queries, width, c) for c in range(3)]
-            + [half_block(queries, LANES, 0)],
-            out_specs=[
-                whole_block(queries, width), whole_block(queries, width),
-                whole_block(queries, LANES),
-            ],
-            scratch_shapes=[pltpu.VMEM((width // LANES, queries, 2 * LANES), jnp.bfloat16)]
-            + [pltpu.VMEM((2, tile, queries), jnp.float32)],
-        ),
-        cost_estimate=attend_cost(heads, queries, queries, width),
-        name="attend_near",
-    )(half.reshape(1), qkv, qkv, qkv, valid)
-
-
-def attend_far(half, qkv, far_kv, far_valid, w_proj, state, heads, tile=512):
-    width, columns = w_proj.shape
-    queries = far_kv.shape[0]
-    return pl.pallas_call(
-        functools.partial(far_kernel, heads, tile),
-        out_shape=jax.ShapeDtypeStruct((queries, columns), jnp.bfloat16),
-        grid_spec=pltpu.PrefetchScalarGridSpec(
-            num_scalar_prefetch=1,
-            grid=(1,),
-            in_specs=[
-                half_block(queries, width, 0),
-                pl.BlockSpec((queries, width), lambda i, half: (0, 0)),
-                pl.BlockSpec((queries, width), lambda i, half: (0, 1)),
-                whole_block(queries, LANES),
-                whole_block(width, columns),
-                whole_block(queries, width), whole_block(queries, width),
-                whole_block(queries, LANES),
-            ],
-            out_specs=whole_block(queries, columns),
-            scratch_shapes=[pltpu.VMEM((width // LANES, queries, 2 * LANES), jnp.bfloat16)]
-            + [pltpu.VMEM((queries, width), jnp.float32)] * 2
-            + [pltpu.VMEM((2, tile, queries), jnp.float32)],
-        ),
-        cost_estimate=attend_cost(heads, queries, queries, width),
-        name="attend_far",
-    )(half.reshape(1), qkv, far_kv, far_kv, far_valid, w_proj, *state)
 
 
 def attend(half, qkv, valid, far_kv, far_valid, w_proj, heads, tile=512):
@@ -603,7 +530,7 @@
             )
             summed = summed + b_ref[c:c + 1, :]
             if c == 0:
-                summed = summed * HD ** (-0.5)
+                summed = summed * (HD ** (-0.5) * LOG2E)
             made[part, c * width:(c + 1) * width] = summed.astype(jnp.bfloat16)
 
     ahead = near - lag
@@ -672,49 +599,297 @@
     )(send, ln_gain.reshape(1, -1), ln_bias.reshape(1, -1), weight, bias)
 
 
-def unpack_kernel(slot_ref, count_ref, made, out_ref, sems):
+def unpack_kernel(slot_ref, count_ref, ext_ref, made, q_ref, k_ref, vt_ref, valid_ref, vals, sems):
     blocks = slot_ref.shape[0]
-    width = out_ref.shape[1] // 3
-
-    def fetch(t):
+    width = q_ref.shape[1]
+    near = (ext_ref.shape[1] - blocks) // 2
+
+    def fetch(t, part, into):
         return pltpu.make_async_copy(
-            made.at[pl.ds(pl.multiple_of(slot_ref[t] * BS, BS), BS)],
-            out_ref.at[pl.ds(pl.multiple_of(t * BS, BS), BS)],
-            sems.at[t],
+            made.at[
+                pl.ds(pl.multiple_of(slot_ref[t] * BS, BS), BS), part * width:(part + 1) * width
+            ],
+            into.at[pl.ds(pl.multiple_of(t * BS, BS), BS)],
+            sems.at[part, t],
         )
 
     def begin(t, carry):
-        fetch(t).start()
+        fetch(t, 2, vals).start()
+        fetch(t, 1, k_ref).start()
+        fetch(t, 0, q_ref).start()
         return carry
 
     lax.fori_loop(0, blocks, begin, 0)
+
+    total = valid_ref.shape[1]
+    spread = (
+        lax.broadcasted_iota(jnp.int32, (ext_ref.shape[1], total), 1) // BS
+        == lax.broadcasted_iota(jnp.int32, (ext_ref.shape[1], total), 0)
+    ).astype(jnp.float32).astype(jnp.bfloat16)
+    rows = valid_ref.shape[0]
+    ext = jnp.broadcast_to(ext_ref[...].astype(jnp.float32), (rows, ext_ref.shape[1]))
+    limit = jnp.dot(ext.astype(jnp.bfloat16), spread, preferred_element_type=jnp.float32)
+    place = (lax.broadcasted_iota(jnp.int32, (rows, total), 1) % BS).astype(jnp.float32)
+    valid_ref[...] = (place < limit).astype(jnp.float32).astype(jnp.bfloat16)
+
+    def arrive_values(t, carry):
+        fetch(t, 2, vals).wait()
+        return carry
+
+    lax.fori_loop(0, blocks, arrive_values, 0)
+    step = 256
+    for i in range(blocks * BS // step):
+        part = slice(i * step, (i + 1) * step)
+        own = valid_ref[0:1, near * BS + i * step:near * BS + (i + 1) * step].astype(jnp.float32)
+        turned = jnp.transpose(vals[part, :].astype(jnp.float32))
+        vt_ref[:, part] = (turned * own).astype(jnp.bfloat16)
+
     row_index = lax.broadcasted_iota(jnp.int32, (BS, width), 0)
 
     def mask(t, carry):
-        fetch(t).wait()
+        fetch(t, 1, k_ref).wait()
         into = pl.ds(pl.multiple_of(t * BS, BS), BS)
-        live = row_index < count_ref[t]
-        keys = out_ref[into, width:2 * width].astype(jnp.float32)
-        out_ref[into, width:2 * width] = jnp.where(live, keys, keys[0:1, :]).astype(jnp.bfloat16)
-        vals = out_ref[into, 2 * width:].astype(jnp.float32)
-        out_ref[into, 2 * width:] = jnp.where(live, vals, 0.0).astype(jnp.bfloat16)
+        keys = k_ref[into, :].astype(jnp.float32)
+        live = row_index < count_ref[near + t]
+        k_ref[into, :] = jnp.where(live, keys, keys[0:1, :]).astype(jnp.bfloat16)
         return carry
 
     lax.fori_loop(0, blocks, mask, 0, unroll=4)
 
-
-def unpack_blocks(made, slot_table, own_counts):
+    def arrive_queries(t, carry):
+        fetch(t, 0, q_ref).wait()
+        return carry
+
+    lax.fori_loop(0, blocks, arrive_queries, 0)
+
+
+def unpack_blocks(made, slot_table, ext_counts):
     blocks = slot_table.shape[0]
+    width = made.shape[1] // 3
+    rows = blocks * BS
     vmem = pl.BlockSpec(memory_space=pltpu.VMEM)
     smem = pl.BlockSpec(memory_space=pltpu.SMEM)
     return pl.pallas_call(
         unpack_kernel,
-        out_shape=jax.ShapeDtypeStruct((blocks * BS, made.shape[1]), jnp.bfloat16),
-        in_specs=[smem, smem, pl.BlockSpec(memory_space=pl.ANY)],
+        out_shape=[
+            jax.ShapeDtypeStruct((rows, width), jnp.bfloat16),
+            jax.ShapeDtypeStruct((rows, width), jnp.bfloat16),
+            jax.ShapeDtypeStruct((width, rows), jnp.bfloat16),
+            jax.ShapeDtypeStruct((HD, ext_counts.shape[0] * BS), jnp.bfloat16),
+        ],
+        in_specs=[smem, smem, vmem, pl.BlockSpec(memory_space=pl.ANY)],
+        out_specs=[vmem] * 4,
+        scratch_shapes=[
+            pltpu.VMEM((rows, width), jnp.bfloat16), pltpu.SemaphoreType.DMA((3, blocks)),
+        ],
+        name="unpack_blocks",
+    )(slot_table, ext_counts, ext_counts.reshape(1, -1), made)
+
+
+def patch_kernel(
+    regions, tile, group, chunk,
+    q_ref, k_ref, vt_ref, valid_ref, w_ref, b_ref, out_ref,
+    kh, vth, w_other, acc, peaks, att, att_in, ahead, ahead_peak,
+    send_sem, recv_sem, side_sem,
+):
+    r = lax.axis_index("region")
+    h = lax.axis_index("head")
+    other = 1 - h
+    half = kh.shape[1]
+    width = q_ref.shape[1]
+    heads = width // HD
+    per = LANES // HD
+    tiles = half // tile
+    trips = heads // group
+    lane = lax.broadcasted_iota(jnp.int32, (1, LANES), 1)
+
+    def toward(a):
+        return lax.rem(r + 1 - 2 * a + regions, regions)
+
+    barrier = pltpu.get_barrier_semaphore()
+    for a in range(2):
+        pl.semaphore_signal(
+            barrier, inc=1, device_id={"region": toward(a)}, device_id_type=MESH
+        )
+    pl.semaphore_signal(barrier, inc=1, device_id={"head": other}, device_id_type=MESH)
+    pl.semaphore_wait(barrier, 3)
+
+    def start_of(a):
+        return pl.multiple_of(a * half, half)
+
+    def halo(a, which):
+        rows = pl.ds(start_of(1 - a), half)
+        source = k_ref.at[rows, :] if which == 0 else vt_ref.at[:, rows]
+        target = kh.at[a] if which == 0 else vth.at[a]
+        return pltpu.make_async_remote_copy(
+            src_ref=source, dst_ref=target,
+            send_sem=send_sem.at[which, a], recv_sem=recv_sem.at[which, a],
+            device_id={"region": toward(a)}, device_id_type=MESH,
+        )
+
+    def across(source, target, slot):
+        return pltpu.make_async_remote_copy(
+            src_ref=source, dst_ref=target,
+            send_sem=side_sem.at[0, slot], recv_sem=side_sem.at[1, slot],
+            device_id={"head": other}, device_id_type=MESH,
+        )
+
+    weights = across(w_ref, w_other, 0)
+    halo(other, 0).start()
+    halo(other, 1).start()
+    halo(h, 0).start()
+    halo(h, 1).start()
+    weights.start()
+
+    def score(slot, a, n, i, keys):
+        columns = pl.ds(pl.multiple_of(n // per * LANES, LANES), LANES)
+        mine = (lane // HD == n % per).astype(jnp.float32).astype(jnp.bfloat16)
+        queries = q_ref[pl.ds(pl.multiple_of(a * half + i * tile, tile), tile), columns] * mine
+        top = None
+        for first in range(0, half, chunk):
+            scores = lax.dot_general(
+                keys(a, first, columns), queries, (((1,), (1,)), ((), ())),
+                preferred_element_type=jnp.float32,
+            )
+            ahead[slot, first:first + chunk] = scores
+            part = jnp.max(scores.reshape(chunk // 8, 8, tile), axis=0)
+            top = part if top is None else jnp.maximum(top, part)
+        ahead_peak[slot] = jnp.broadcast_to(jnp.max(top, axis=0, keepdims=True), (8, tile))
+
+    def weigh(slot, a, n, peak, vals, flags):
+        total = None
+        rows = pl.ds(pl.multiple_of(n * HD, HD), HD)
+        for first in range(0, half, chunk):
+            scores = ahead[slot, first:first + chunk].reshape(chunk // 8, 8, tile)
+            expo = jnp.exp2(scores - peak[None]).reshape(chunk, tile).astype(jnp.bfloat16)
+            left = jnp.concatenate([vals(a, rows, first), flags(a, first)], axis=0)
+            part = jnp.dot(left, expo, preferred_element_type=jnp.float32)
+            total = part if total is None else total + part
+        return total
+
+    def run(trip_from, trip_to, limit, where, keys, use):
+        def body(trip, carry):
+            units = [(u, i) for u in range(group) for i in range(tiles)]
+            for turn, (u, i) in enumerate(units):
+                if turn + 1 < len(units):
+                    v, j = units[turn + 1]
+                    a, n = where(trip)
+                    score((turn + 1) % 2, a, n + v, j, keys)
+                else:
+                    a, n = where(jnp.minimum(trip + 1, limit - 1))
+                    score((turn + 1) % 2, a, n, 0, keys)
+                a, n = where(trip)
+                use(turn % 2, a, n + u, i)
+            return carry
+
+        lax.fori_loop(trip_from, trip_to, body, 0)
+
+    def near_keys(a, first, columns):
+        return k_ref[pl.ds(pl.multiple_of(a * half + first, chunk), chunk), columns]
+
+    def near_vals(a, rows, first):
+        return vt_ref[rows, pl.ds(pl.multiple_of(a * half + first, chunk), chunk)]
+
+    def near_flags(a, first):
+        return valid_ref[:, pl.ds(pl.multiple_of((a + 1) * half + first, chunk), chunk)]
+
+    def far_keys(a, first, columns):
+        return kh[a, first:first + chunk, columns]
+
+    def far_vals(a, rows, first):
+        return vth[a, rows, first:first + chunk]
+
+    def far_flags(a, first):
+        return valid_ref[:, pl.ds(pl.multiple_of(a * 3 * half + first, chunk), chunk)]
+
+    def near_use(slot, a, n, i):
+        peak = ahead_peak[slot]
+        columns = slice(i * tile, (i + 1) * tile)
+        acc[a, n, :, columns] = weigh(slot, a, n, peak, near_vals, near_flags)
+        peaks[a, n, :, columns] = peak
+
+    def far_use(slot, a, n, i):
+        columns = slice(i * tile, (i + 1) * tile)
+        old = peaks[a, n, :, columns]
+        peak = jnp.maximum(ahead_peak[slot], old)
+        keep = jnp.exp2(old - peak)
+        total = weigh(slot, a, n, peak, far_vals, far_flags)
+        before = acc[a, n, :, columns].reshape(2 * HD // 8, 8, tile)
+        total = total + (before * keep[None]).reshape(2 * HD, tile)
+        att[a, pl.ds(pl.multiple_of(n * HD, HD), HD), columns] = (
+            total[:HD] / total[HD:]
+        ).astype(jnp.bfloat16)
+
+    def near_where(trip):
+        late = lax.div(trip, trips)
+        return lax.rem(other + late, 2), lax.rem(trip, trips) * group
+
+    score(0, other, 0, 0, near_keys)
+    run(0, 2 * trips, 2 * trips, near_where, near_keys, near_use)
+
+    halo(other, 0).wait_recv()
+    halo(other, 1).wait_recv()
+    score(0, other, 0, 0, far_keys)
+    run(0, trips, trips, lambda trip: (other, trip * group), far_keys, far_use)
+
+    halo(h, 0).wait_recv()
+    halo(h, 1).wait_recv()
+    score(0, h, 0, 0, far_keys)
+    swap_att = across(att.at[other], att_in, 1)
+    run(0, 1, trips, lambda trip: (h, trip * group), far_keys, far_use)
+    swap_att.start()
+    run(1, trips, trips, lambda trip: (h, trip * group), far_keys, far_use)
+
+    def share(attended, weight):
+        return lax.dot_general(
+            attended, weight, (((0,), (0,)), ((), ())), preferred_element_type=jnp.float32
+        ).astype(jnp.bfloat16).astype(jnp.float32)
+
+    flags = valid_ref[:, pl.ds(pl.multiple_of((h + 1) * half, half), half)]
+    ones = jnp.full((HD, out_ref.shape[1]), 1.0 / HD, jnp.bfloat16)
+    own = share(att[h], w_ref[...]) + b_ref[...]
+    live = lax.dot_general(
+        flags, ones, (((0,), (0,)), ((), ())), preferred_element_type=jnp.float32
+    )
+    weights.wait_recv()
+    swap_att.wait_recv()
+    update = own + share(att_in[...], w_other[...])
+    out_ref[...] = jnp.where(live > 0.5, update, 0.0).astype(jnp.bfloat16)
+    weights.wait_send()
+    swap_att.wait_send()
+    for a in range(2):
+        for which in range(2):
+            halo(a, which).wait_send()
+
+
+def attend_patches(q, k, vt, valid, w_proj, b_proj, regions, tile=256, group=4, chunk=256):
+    rows, width = q.shape
+    half = rows // 2
+    heads = width // HD
+    columns = w_proj.shape[1]
+    vmem = pl.BlockSpec(memory_space=pltpu.VMEM)
+    return pl.pallas_call(
+        functools.partial(patch_kernel, regions, tile, group, chunk),
+        out_shape=jax.ShapeDtypeStruct((half, columns), jnp.bfloat16),
+        in_specs=[vmem] * 6,
         out_specs=vmem,
-        scratch_shapes=[pltpu.SemaphoreType.DMA((blocks,))],
-        name="unpack_blocks",
-    )(slot_table, own_counts, made)
+        scratch_shapes=[
+            pltpu.VMEM((2, half, width), jnp.bfloat16),
+            pltpu.VMEM((2, width, half), jnp.bfloat16),
+            pltpu.VMEM((width, columns), jnp.bfloat16),
+            pltpu.VMEM((2, heads, 2 * HD, half), jnp.float32),
+            pltpu.VMEM((2, heads, 8, half), jnp.float32),
+            pltpu.VMEM((2, width, half), jnp.bfloat16),
+            pltpu.VMEM((width, half), jnp.bfloat16),
+            pltpu.VMEM((2, half, tile), jnp.float32),
+            pltpu.VMEM((2, 8, tile), jnp.float32),
+            pltpu.SemaphoreType.DMA((2, 2)),
+            pltpu.SemaphoreType.DMA((2, 2)),
+            pltpu.SemaphoreType.DMA((2, 2)),
+        ],
+        compiler_params=pltpu.CompilerParams(collective_id=2, has_side_effects=True),
+        name="attend_patches",
+    )(q, k, vt, valid, w_proj, b_proj.reshape(1, -1))
 
 
 def shards(points, ln_gain, ln_bias, w_qkv, b_qkv, w_proj, b_proj, counts, hilbert_pos):
@@ -775,55 +950,27 @@
         made = swap(
             send, ln_gain, ln_bias, jnp.transpose(w_qkv, (1, 0, 2)), b_qkv, regions
         )
-        qkv = unpack_blocks(made, slot_table, own_counts)
-    else:
-        packed = pack_blocks(points, ln_gain, ln_bias, h, pack_table, heads_axis)
-        recv = exchange(packed, regions, heads_axis)
-        weight = jnp.pad(w_qkv, ((0, 0), (0, 0), (0, pad))).reshape(model_width, 3 * width)
-        bias = jnp.pad(b_qkv, ((0, 0), (0, pad))).reshape(3 * width)
-        qkv = project(recv, slot_table, own_counts, valid, weight, bias)
-
-    if heads_axis == 2:
-        order = (1 - h, h)
-        flat = lambda a, b: (a % regions) * 2 + b
-        fars = []
-        for turn in range(2):
-            pairs = []
-            for i in range(regions):
-                for b in range(2):
-                    upper = (1 - b if turn == 0 else b) == 1
-                    pairs.append((flat(i + 1 if upper else i - 1, b), flat(i, b)))
-            start = (1 - order[turn]) * half_rows
-            piece = lax.dynamic_slice(qkv, (start, width), (half_rows, 2 * width))
-            fars.append(lax.ppermute(piece, ("region", "head"), pairs))
-        partials = []
-        for turn in range(2):
-            half = order[turn]
-            far_valid = lax.dynamic_slice(
-                valid_ext, (half * (rows + half_rows), 0), (half_rows, LANES)
-            )
-            if turn == 0:
-                state = attend_near(half, qkv, valid, width, half_rows, heads)
-                partials.append(
-                    attend_far(half, qkv, fars[0], far_valid, w_out, state, heads)
-                )
-                arrived = lax.ppermute(partials[0], "head", [(0, 1), (1, 0)])
-            else:
-                partials.append(attend(half, qkv, valid, fars[1], far_valid, w_out, heads))
-        summed_rows = partials[1].astype(jnp.float32) + arrived.astype(jnp.float32)
-    else:
-        up = [(i, (i + 1) % regions) for i in range(regions)]
-        down = [(j, i) for i, j in up]
-        kv = qkv[:, width:]
-        before = lax.ppermute(kv[rows - half_rows:], "region", up)
-        after = lax.ppermute(kv[:half_rows], "region", down)
-        partials = [
-            attend(jnp.int32(0), qkv, valid, before, valid_ext[:half_rows], w_out, heads),
-            attend(jnp.int32(1), qkv, valid, after, valid_ext[rows + half_rows:], w_out, heads),
-        ]
-        summed_rows = lax.psum_scatter(
-            jnp.concatenate(partials, axis=0), "head", scatter_dimension=0, tiled=True
-        ).astype(jnp.float32)
+        q, k, vt, flags = unpack_blocks(made, slot_table, ext_counts)
+        return attend_patches(q, k, vt, flags, w_proj, b_proj, regions)
+
+    packed = pack_blocks(points, ln_gain, ln_bias, h, pack_table, heads_axis)
+    recv = exchange(packed, regions, heads_axis)
+    weight = jnp.pad(w_qkv, ((0, 0), (0, 0), (0, pad))).reshape(model_width, 3 * width)
+    bias = jnp.pad(b_qkv, ((0, 0), (0, pad))).reshape(3 * width)
+    qkv = project(recv, slot_table, own_counts, valid, weight, bias)
+
+    up = [(i, (i + 1) % regions) for i in range(regions)]
+    down = [(j, i) for i, j in up]
+    kv = qkv[:, width:]
+    before = lax.ppermute(kv[rows - half_rows:], "region", up)
+    after = lax.ppermute(kv[:half_rows], "region", down)
+    partials = [
+        attend(jnp.int32(0), qkv, valid, before, valid_ext[:half_rows], w_out, heads),
+        attend(jnp.int32(1), qkv, valid, after, valid_ext[rows + half_rows:], w_out, heads),
+    ]
+    summed_rows = lax.psum_scatter(
+        jnp.concatenate(partials, axis=0), "head", scatter_dimension=0, tiled=True
+    ).astype(jnp.float32)
     share = rows // heads_axis
     share_valid = lax.dynamic_slice(valid, (h * share, 0), (share, LANES))[:, :1] > 0
     return jnp.where(share_valid, summed_rows + b_proj, 0.0).astype(jnp.bfloat16)

time: 97 us -> 86.7 us (0.89)
  starting transfers between devices: 9.53 us -> 0 us
  Pallas kernels: 76.8 us -> 80.5 us
  local copies, waits for them, and re-layouts: 4.71 us -> 1.87 us
  other arithmetic: 5.41 us -> 3.82 us
    ppermute x3 -> x0, starting transfers between devices: 9.53 us -> none  [the longest x2 8.2 us: shards(): fars.append(lax.ppermute(piece, ('region', 'head'), pairs))]
    pallas_call x4 -> x2, Pallas kernels: 35.4 us -> 39.1 us  [the longest x1 34.3 us: attend_patches(): pl.pallas_call(functools.partial(patch_kernel, regions, tile, group, chun...]
    broadcast_in_dim x3 -> x0, local copies, waits for them, and re-layouts: 2.58 us -> none  [shards(): jnp.broadcast_to(valid_ext, (blocks + 2 * half_blocks, BS, LANES))]
    convert_element_type x2 -> x0, other arithmetic: 2.13 us -> none  [the longest x1 2.06 us: shards(): jnp.where(share_valid, summed_rows + b_proj, 0.0).astype(jnp.bfloat16)]
    unnamed x6 -> x1, local copies, waits for them, and re-layouts: 0.01 us -> 1.87 us
    dynamic_slice x2 -> x0, local copies, waits for them, and re-layouts: 1.36 us -> none  [the longest x1 1.28 us: shards(): piece = lax.dynamic_slice(qkv, (start, width), (half_rows, 2 * width))]
  transfers between devices with their start and end apart: 3 -> 0, of which waited for: 0 -> 0; matrix products, arithmetic and copies ran while one was open for 3% -> 0% of each run, Pallas kernels for 33% -> 0%
where the time goes in v2:
time: 86.7 us; the launch traced here: 86.2 us
  Pallas kernels  80.5 us (93%)
  other arithmetic  3.82 us (4%)
  local copies, waits for them, and re-layouts  1.87 us (2%)
    pallas_call x1, Pallas kernels, swap(): pl.pallas_call(functools.partial(swap_kernel, regions, regions // 4), out...  38.5 us
    pallas_call x1, Pallas kernels, attend_patches(): pl.pallas_call(functools.partial(patch_kernel, regions, tile, group, chun...  34.3 us
    pallas_call x1, Pallas kernels, unpack_blocks(): pl.pallas_call(unpack_kernel, out_shape=[jax.ShapeDtypeStruct((rows, widt...  4.84 us
    pallas_call x1, Pallas kernels, gather_blocks(): pl.pallas_call(functools.partial(gather_kernel, slots), out_shape=jax.Sha...  2.84 us
    unnamed x1, local copies, waits for them, and re-layouts  1.87 us

profile of v2, /device:TPU:0, one launch (start us, length us, event | category | flops | bytes accessed | tf_op | source)
XLA Modules:
  0.0 86.2 jit_solution(6526915442921919146)
XLA Ops:
  0.0 0.7 fusion.3
  0.7 1.5 %select_reduce_fusion.count_ref = s32[64]{0:T(128)} fusion(s32[512]{0:T(512)} %param.16, s32[64]{0:T(128)S(1)} %and_select_fusion.1, s32[512]{0:T(512)} %pos_ref.1), kind=kLoop, calls=%fused_computation | loop fusion | flops 98240 | bytes 4608 | tf_op jit(solution)/shard_map/reduce_sum | solution.py:927
  2.2 0.8 broadcast_compare_fusion
  2.9 0.1 select_reduce_fusion.1
  3.1 0.2 convert_reduce_fusion
  3.3 0.6 multiply_add_fusion.slot_ref
  3.8 2.8 %gather_blocks.1.send = bf16[2,2048,256]{2,1,0:T(8,128)(2,1)} custom-call(s32[512]{0:T(512)} %pos_ref.1, bf16[1024,512]{1,0:T(8,128)(2,1)} %x_ref.1), custom_call_target="tpu_custom_call" | custom-call | tf_op jit(solution)/shard_map/gather_blocks/pallas_call | solution.py:399
  6.7 38.5 %swap.1.made = bf16[2048,768]{1,0:T(8,128)(2,1)} custom-call(bf16[2,2048,256]{2,1,0:T(8,128)(2,1)} %gather_blocks.1.send, f32[1,512]{1,0:T(1,128)} %bitcast.7, f32[1,512]{1,0:T(1,128)} %bitcast.8, bf16[3,512,256]{2,1,0:T(8,128)(2,1)} %bitcast.5, f32[3,256]{1,0:T(4,128)} %b_ref.1), custom_call_target="tpu_custom_call" | custom-call | tf_op jit(solution)/shard_map/swap/pallas_call | solution.py:586
  45.2 4.8 %unpack_blocks.1 = (bf16[1024,256]{1,0:T(8,128)(2,1)}, bf16[1024,256]{1,0:T(8,128)(2,1)}, bf16[256,1024]{1,0:T(8,128)(2,1)}, bf16[16,2048]{1,0:T(8,128)(2,1)}) custom-call(s32[32]{0:T(128)} %multiply_add_fusion.slot_ref, s32[64]{0:T(128)} %select_reduce_fusion.count_ref, s32[1,64]{1,0:T(1,128)} %bitcast.6, bf16[2048,768]{1,0:T(8,128)(2,1)} %swap.1.made), custom_call_target="tpu_custom_call" | custom-call | tf_op jit(solution)/shard_map/unpack_blocks/pallas_call | solution.py:672
  50.0 34.3 %attend_patches.1 = bf16[512,512]{1,0:T(8,128)(2,1)} custom-call(bf16[1024,256]{1,0:T(8,128)(2,1)} %get-tuple-element.9.q_ref, bf16[1024,256]{1,0:T(8,128)(2,1)} %get-tuple-element.10.k_ref, bf16[256,1024]{1,0:T(8,128)(2,1)} %get-tuple-element.11.vt_ref, bf16[16,2048]{1,0:T(8,128)(2,1)} %get-tuple-element.12.valid_ref, bf16[256,512]{1,0:T(8,128)(2,1)} %w_ref.1, ...), custom_call_target="tpu_custom_call" | custom-call | tf_op jit(solution)/shard_map/attend_patches/pallas_call | solution.py:871
  84.3 1.9 %copy.11 = bf16[512,512]{1,0:T(8,128)(2,1)} copy(bf16[512,512]{1,0:T(8,128)(2,1)} %attend_patches.1) | data formatting | bytes 1048576
  (3 shorter events, 0.0 us)

commit v3 on v2

--- a/solution.py
+++ b/solution.py
@@ -410,8 +410,8 @@
 
 def swap_kernel(
     regions, near,
-    send, gain_ref, bias_ref, w_ref, b_ref, made,
-    recv, send_sem, recv_sem, relay_sem,
+    send, gain_ref, bias_ref, w_ref, b_ref, out_ref,
+    recv, made, send_sem, recv_sem, relay_sem, leave_sem,
 ):
     r = lax.axis_index("region")
     h = lax.axis_index("head")
@@ -420,9 +420,10 @@
     piece = recv.shape[2]
     width = w_ref.shape[2]
     seat = lax.rem(r, near)
-    base = r - seat
-    far = regions - near
-    lag = 2
+    level = lax.div(r, near)
+    high = lax.div(level, 2)
+    low = lax.rem(level, 2)
+    whole = 2 * near
 
     barrier = pltpu.get_barrier_semaphore()
 
@@ -474,37 +475,33 @@
             send.at[part, rows(r)], recv.at[part, rows(r)], recv_sem.at[part, r]
         )
 
-    def near_target(j):
-        return base + lax.rem(seat + j, near)
-
-    def far_target(j):
-        group = lax.div(j, near)
-        return lax.rem(base + near * (group + 1), regions) + lax.rem(seat + lax.rem(j, near), near)
-
-    def near_source(j):
-        return base + lax.rem(seat + near - j, near)
-
-    def far_source(j):
-        group = lax.div(j, near)
-        return lax.rem(base + regions - near * (group + 1), regions) + lax.rem(
-            seat + near - lax.rem(j, near), near
-        )
+    def target(i):
+        group = lax.div(i, near)
+        beyond = lax.div(group, 2)
+        there = 2 * lax.rem(high + beyond, 2) + lax.rem(low + group, 2)
+        return there * near + lax.rem(seat + i, near)
+
+    def source(i):
+        group = lax.div(i, near)
+        beyond = lax.div(group, 2)
+        inner = (1 - beyond) * low + beyond * high + group
+        there = 2 * lax.rem(high + beyond, 2) + lax.rem(inner, 2)
+        return there * near + lax.rem(seat + regions - i, near)
+
+    def push_whole(i, carry):
+        t = target(i)
+        to_region(t, h).start()
+        to_region(t, other).start()
+        return carry
+
+    def push_part(i, carry):
+        to_region(target(i), h).start()
+        return carry
 
     keep(0).start()
     keep(1).start()
-
-    def push_near(j, carry):
-        t = near_target(j)
-        to_region(t, 0).start()
-        to_region(t, 1).start()
-        return carry
-
-    def push_far(j, carry):
-        to_region(far_target(j), h).start()
-        return carry
-
-    lax.fori_loop(1, near, push_near, 0)
-    lax.fori_loop(0, far, push_far, 0)
+    lax.fori_loop(1, whole, push_whole, 0)
+    lax.fori_loop(whole, regions, push_part, 0)
 
     def project(s):
         part = rows(s)
@@ -533,50 +530,64 @@
                 summed = summed * (HD ** (-0.5) * LOG2E)
             made[part, c * width:(c + 1) * width] = summed.astype(jnp.bfloat16)
 
-    ahead = near - lag
-
-    def forward(j):
-        s = far_source(j)
+    def leave(s):
+        return pltpu.make_async_copy(made.at[rows(s)], out_ref.at[rows(s)], leave_sem.at[s])
+
+    def forward(i):
+        s = source(i)
         arrival(s, h).wait_recv()
         relay(s).start()
 
+    last = regions - near
+
     def close(i, carry):
-        @pl.when(i >= lag)
+        @pl.when((i >= 1) & (i < 1 + near))
         def _():
-            forward(i - lag)
-
-        s = near_source(i)
+            forward(whole + i - 1)
+
+        s = source(i)
         arrival(s, 0).wait_recv()
         arrival(s, 1).wait_recv()
         project(s)
-        return carry
-
-    def distant(j, carry):
-        @pl.when(j < far - ahead)
+        leave(s).start()
+        return carry
+
+    def distant(i, carry):
+        @pl.when(i == last - 2)
         def _():
-            forward(j + ahead)
-
-        s = far_source(j)
+            forward(last)
+
+        @pl.when((i >= last) & (i < regions - 1))
+        def _():
+            forward(i + 1)
+
+        s = source(i)
         arrival(s, other).wait_recv()
         project(s)
-        return carry
-
-    lax.fori_loop(0, near, close, 0)
-    lax.fori_loop(0, far, distant, 0)
-
-    def drain_near(j, carry):
-        t = near_target(j)
-        to_region(t, 0).wait_send()
-        to_region(t, 1).wait_send()
-        return carry
-
-    def drain_far(j, carry):
-        to_region(far_target(j), h).wait_send()
-        relay(far_source(j)).wait_send()
-        return carry
-
-    lax.fori_loop(1, near, drain_near, 0)
-    lax.fori_loop(0, far, drain_far, 0)
+        leave(s).start()
+        return carry
+
+    lax.fori_loop(0, whole, close, 0)
+    lax.fori_loop(whole, regions, distant, 0)
+
+    def drain_whole(i, carry):
+        t = target(i)
+        to_region(t, h).wait_send()
+        to_region(t, other).wait_send()
+        return carry
+
+    def drain_part(i, carry):
+        to_region(target(i), h).wait_send()
+        relay(source(i)).wait_send()
+        return carry
+
+    def drain_leave(i, carry):
+        leave(i).wait()
+        return carry
+
+    lax.fori_loop(1, whole, drain_whole, 0)
+    lax.fori_loop(whole, regions, drain_part, 0)
+    lax.fori_loop(0, regions, drain_leave, 0)
 
 
 def swap(send, ln_gain, ln_bias, weight, bias, regions):
@@ -587,11 +598,13 @@
         functools.partial(swap_kernel, regions, regions // 4),
         out_shape=jax.ShapeDtypeStruct((rows, 3 * width), jnp.bfloat16),
         in_specs=[pl.BlockSpec(memory_space=pl.ANY), vmem, vmem, vmem, vmem],
-        out_specs=vmem,
+        out_specs=pl.BlockSpec(memory_space=pl.ANY),
         scratch_shapes=[
             pltpu.VMEM((parts, rows, piece), jnp.bfloat16),
+            pltpu.VMEM((rows, 3 * width), jnp.bfloat16),
             pltpu.SemaphoreType.DMA((parts, regions)),
             pltpu.SemaphoreType.DMA((parts, regions)),
+            pltpu.SemaphoreType.DMA((regions,)),
             pltpu.SemaphoreType.DMA((regions,)),
         ],
         compiler_params=pltpu.CompilerParams(collective_id=1, has_side_effects=True),

time: 86.7 us -> 83.2 us (0.960)
  Pallas kernels: 80.5 us -> 77 us
    pallas_call x1, Pallas kernels: 34.3 us -> 30.7 us  [attend_patches(): pl.pallas_call(functools.partial(patch_kernel, regions, tile, group, chun...]
where the time goes in v3:
time: 83.2 us; the launch traced here: 82.7 us
  Pallas kernels  77 us (93%)
  other arithmetic  3.82 us (5%)
  local copies, waits for them, and re-layouts  1.87 us (2%)
    pallas_call x1, Pallas kernels, swap(): pl.pallas_call(functools.partial(swap_kernel, regions, regions // 4), out...  38.6 us
    pallas_call x1, Pallas kernels, attend_patches(): pl.pallas_call(functools.partial(patch_kernel, regions, tile, group, chun...  30.7 us
    pallas_call x1, Pallas kernels, unpack_blocks(): pl.pallas_call(unpack_kernel, out_shape=[jax.ShapeDtypeStruct((rows, widt...  4.84 us
    pallas_call x1, Pallas kernels, gather_blocks(): pl.pallas_call(functools.partial(gather_kernel, slots), out_shape=jax.Sha...  2.84 us
    unnamed x1, local copies, waits for them, and re-layouts  1.87 us

profile of v3, /device:TPU:0, one launch (start us, length us, event | category | flops | bytes accessed | tf_op | source)
XLA Modules:
  0.0 82.7 jit_solution(8300600117302621300)
XLA Ops:
  0.0 0.7 fusion.3
  0.7 1.5 %select_reduce_fusion.count_ref = s32[64]{0:T(128)} fusion(s32[512]{0:T(512)} %param.16, s32[64]{0:T(128)S(1)} %and_select_fusion.1, s32[512]{0:T(512)} %pos_ref.1), kind=kLoop, calls=%fused_computation | loop fusion | flops 98240 | bytes 4608 | tf_op jit(solution)/shard_map/reduce_sum | solution.py:940
  2.2 0.8 broadcast_compare_fusion
  2.9 0.1 select_reduce_fusion.1
  3.1 0.2 convert_reduce_fusion
  3.3 0.6 multiply_add_fusion.slot_ref
  3.8 2.8 %gather_blocks.1.send = bf16[2,2048,256]{2,1,0:T(8,128)(2,1)} custom-call(s32[512]{0:T(512)} %pos_ref.1, bf16[1024,512]{1,0:T(8,128)(2,1)} %x_ref.1), custom_call_target="tpu_custom_call" | custom-call | tf_op jit(solution)/shard_map/gather_blocks/pallas_call | solution.py:399
  6.7 38.6 %swap.1.made = bf16[2048,768]{1,0:T(8,128)(2,1)} custom-call(bf16[2,2048,256]{2,1,0:T(8,128)(2,1)} %gather_blocks.1.send, f32[1,512]{1,0:T(1,128)} %bitcast.7, f32[1,512]{1,0:T(1,128)} %bitcast.8, bf16[3,512,256]{2,1,0:T(8,128)(2,1)} %bitcast.5, f32[3,256]{1,0:T(4,128)} %b_ref.1), custom_call_target="tpu_custom_call" | custom-call | tf_op jit(solution)/shard_map/swap/pallas_call | solution.py:597
  45.3 4.8 %unpack_blocks.1 = (bf16[1024,256]{1,0:T(8,128)(2,1)}, bf16[1024,256]{1,0:T(8,128)(2,1)}, bf16[256,1024]{1,0:T(8,128)(2,1)}, bf16[16,2048]{1,0:T(8,128)(2,1)}) custom-call(s32[32]{0:T(128)} %multiply_add_fusion.slot_ref, s32[64]{0:T(128)} %select_reduce_fusion.count_ref, s32[1,64]{1,0:T(1,128)} %bitcast.6, bf16[2048,768]{1,0:T(8,128)(2,1)} %swap.1.made), custom_call_target="tpu_custom_call" | custom-call | tf_op jit(solution)/shard_map/unpack_blocks/pallas_call | solution.py:685
  50.1 30.7 %attend_patches.1 = bf16[512,512]{1,0:T(8,128)(2,1)} custom-call(bf16[1024,256]{1,0:T(8,128)(2,1)} %get-tuple-element.9.q_ref, bf16[1024,256]{1,0:T(8,128)(2,1)} %get-tuple-element.10.k_ref, bf16[256,1024]{1,0:T(8,128)(2,1)} %get-tuple-element.11.vt_ref, bf16[16,2048]{1,0:T(8,128)(2,1)} %get-tuple-element.12.valid_ref, bf16[256,512]{1,0:T(8,128)(2,1)} %w_ref.1, ...), custom_call_target="tpu_custom_call" | custom-call | tf_op jit(solution)/shard_map/attend_patches/pallas_call | solution.py:884
  80.9 1.9 %copy.11 = bf16[512,512]{1,0:T(8,128)(2,1)} copy(bf16[512,512]{1,0:T(8,128)(2,1)} %attend_patches.1) | data formatting | bytes 1048576
  (3 shorter events, 0.0 us)

commit v4 on v3

--- a/solution.py
+++ b/solution.py
@@ -372,7 +372,7 @@
     )(half.reshape(1), qkv, qkv, qkv, valid, far_kv, far_kv, far_valid, w_proj)
 
 
-def gather_kernel(slots, pos_ref, x_ref, out_ref, taken):
+def gather_kernel(slots, pos_ref, x_ref, out_ref, taken, sems):
     rows, depth = x_ref.shape
     parts, _, width = out_ref.shape
     blocks = rows // BS
@@ -380,17 +380,30 @@
     for d in range(taken.shape[0]):
         taken[d] = 0
 
+    def move(i, part, into):
+        return pltpu.make_async_copy(
+            x_ref.at[
+                pl.ds(pl.multiple_of(i * BS, BS), BS), part * width:(part + 1) * width
+            ],
+            out_ref.at[part, pl.ds(pl.multiple_of(into * BS, BS), BS)],
+            sems.at[part, i],
+        )
+
     def place(i, carry):
         target = lax.div(pos_ref[first + i], blocks)
         used = taken[target]
         taken[target] = used + 1
-        into = pl.ds(pl.multiple_of((target * slots + used) * BS, BS), BS)
-        source = pl.ds(pl.multiple_of(i * BS, BS), BS)
         for part in range(parts):
-            out_ref[part, into, :] = x_ref[source, part * width:(part + 1) * width]
+            move(i, part, target * slots + used).start()
+        return carry
+
+    def settle(i, carry):
+        for part in range(parts):
+            move(i, part, i).wait()
         return carry
 
     lax.fori_loop(0, blocks, place, 0, unroll=4)
+    lax.fori_loop(0, blocks, settle, 0, unroll=4)
 
 
 def gather_blocks(points, hilbert_pos, regions, slots, parts):
@@ -402,15 +415,50 @@
             (parts, regions * slots * BS, depth // parts), jnp.bfloat16
         ),
         in_specs=[pl.BlockSpec(memory_space=pltpu.SMEM), vmem],
-        out_specs=vmem,
-        scratch_shapes=[pltpu.SMEM((regions,), jnp.int32)],
+        out_specs=pl.BlockSpec(memory_space=pl.ANY),
+        scratch_shapes=[
+            pltpu.SMEM((regions,), jnp.int32), pltpu.SemaphoreType.DMA((parts, rows // BS)),
+        ],
         name="gather_blocks",
     )(hilbert_pos, points)
 
 
+def tabulate(slots, r, pos_ref, amount_ref, slot_ref, count_ref):
+    total = pos_ref.shape[1]
+    rows = 8
+    span = slot_ref.shape[1]
+    blocks = slots[1]
+    position = jnp.broadcast_to(pos_ref[...], (rows, total))
+    lane = lax.broadcasted_iota(jnp.int32, (rows, total), 1)
+    within = lax.rem(lane, blocks)
+    goal = lax.div(position, blocks)
+    rank = jnp.zeros((rows, total), jnp.int32)
+    for k in range(1, blocks):
+        same = (pltpu.roll(goal, k, 1) == goal) & (within >= k)
+        rank = rank + same.astype(jnp.int32)
+    slot = (lax.div(lane, blocks) * slots[0] + rank).astype(jnp.float32).astype(jnp.bfloat16)
+    amount = jnp.broadcast_to(amount_ref[...], (rows, total)).astype(jnp.float32)
+    wanted = lax.rem(
+        lax.broadcasted_iota(jnp.int32, (span, total), 0)
+        + (r * blocks - (span - blocks) // 2 + total),
+        total,
+    )
+    found = (jnp.broadcast_to(pos_ref[...], (span, total)) == wanted).astype(jnp.float32)
+    found = found.astype(jnp.bfloat16)
+
+    def pick(values):
+        picked = lax.dot_general(
+            values, found, (((1,), (1,)), ((), ())), preferred_element_type=jnp.float32
+        )
+        return picked[0:1, :].astype(jnp.int32)
+
+    slot_ref[...] = pick(slot)
+    count_ref[...] = pick(amount.astype(jnp.bfloat16))
+
+
 def swap_kernel(
-    regions, near,
-    send, gain_ref, bias_ref, w_ref, b_ref, out_ref,
+    regions, near, slots,
+    send, pos_ref, amount_ref, gain_ref, bias_ref, w_ref, b_ref, out_ref, slot_ref, count_ref,
     recv, made, send_sem, recv_sem, relay_sem, leave_sem,
 ):
     r = lax.axis_index("region")
@@ -567,6 +615,7 @@
         leave(s).start()
         return carry
 
+    tabulate(slots, r, pos_ref, amount_ref, slot_ref, count_ref)
     lax.fori_loop(0, whole, close, 0)
     lax.fori_loop(whole, regions, distant, 0)
 
@@ -590,15 +639,19 @@
     lax.fori_loop(0, regions, drain_leave, 0)
 
 
-def swap(send, ln_gain, ln_bias, weight, bias, regions):
+def swap(send, hilbert_pos, counts, ln_gain, ln_bias, weight, bias, regions, slots, blocks, near):
     parts, rows, piece = send.shape
     width = weight.shape[2]
     vmem = pl.BlockSpec(memory_space=pltpu.VMEM)
     return pl.pallas_call(
-        functools.partial(swap_kernel, regions, regions // 4),
-        out_shape=jax.ShapeDtypeStruct((rows, 3 * width), jnp.bfloat16),
-        in_specs=[pl.BlockSpec(memory_space=pl.ANY), vmem, vmem, vmem, vmem],
-        out_specs=pl.BlockSpec(memory_space=pl.ANY),
+        functools.partial(swap_kernel, regions, regions // 4, (slots, blocks)),
+        out_shape=[
+            jax.ShapeDtypeStruct((rows, 3 * width), jnp.bfloat16),
+            jax.ShapeDtypeStruct((1, blocks + 2 * near), jnp.int32),
+            jax.ShapeDtypeStruct((1, blocks + 2 * near), jnp.int32),
+        ],
+        in_specs=[pl.BlockSpec(memory_space=pl.ANY)] + [vmem] * 6,
+        out_specs=[pl.BlockSpec(memory_space=pl.ANY), vmem, vmem],
         scratch_shapes=[
             pltpu.VMEM((parts, rows, piece), jnp.bfloat16),
             pltpu.VMEM((rows, 3 * width), jnp.bfloat16),
@@ -609,18 +662,21 @@
         ],
         compiler_params=pltpu.CompilerParams(collective_id=1, has_side_effects=True),
         name="swap",
-    )(send, ln_gain.reshape(1, -1), ln_bias.reshape(1, -1), weight, bias)
+    )(
+        send, hilbert_pos.reshape(1, -1), counts.reshape(1, -1), ln_gain.reshape(1, -1),
+        ln_bias.reshape(1, -1), weight, bias,
+    )
 
 
 def unpack_kernel(slot_ref, count_ref, ext_ref, made, q_ref, k_ref, vt_ref, valid_ref, vals, sems):
-    blocks = slot_ref.shape[0]
+    blocks = q_ref.shape[0] // BS
     width = q_ref.shape[1]
     near = (ext_ref.shape[1] - blocks) // 2
 
     def fetch(t, part, into):
         return pltpu.make_async_copy(
             made.at[
-                pl.ds(pl.multiple_of(slot_ref[t] * BS, BS), BS), part * width:(part + 1) * width
+                pl.ds(pl.multiple_of(slot_ref[0, near + t] * BS, BS), BS), part * width:(part + 1) * width
             ],
             into.at[pl.ds(pl.multiple_of(t * BS, BS), BS)],
             sems.at[part, t],
@@ -663,7 +719,7 @@
         fetch(t, 1, k_ref).wait()
         into = pl.ds(pl.multiple_of(t * BS, BS), BS)
         keys = k_ref[into, :].astype(jnp.float32)
-        live = row_index < count_ref[near + t]
+        live = row_index < count_ref[0, near + t]
         k_ref[into, :] = jnp.where(live, keys, keys[0:1, :]).astype(jnp.bfloat16)
         return carry
 
@@ -676,8 +732,7 @@
     lax.fori_loop(0, blocks, arrive_queries, 0)
 
 
-def unpack_blocks(made, slot_table, ext_counts):
-    blocks = slot_table.shape[0]
+def unpack_blocks(made, slot_table, ext_counts, blocks):
     width = made.shape[1] // 3
     rows = blocks * BS
     vmem = pl.BlockSpec(memory_space=pltpu.VMEM)
@@ -688,7 +743,7 @@
             jax.ShapeDtypeStruct((rows, width), jnp.bfloat16),
             jax.ShapeDtypeStruct((rows, width), jnp.bfloat16),
             jax.ShapeDtypeStruct((width, rows), jnp.bfloat16),
-            jax.ShapeDtypeStruct((HD, ext_counts.shape[0] * BS), jnp.bfloat16),
+            jax.ShapeDtypeStruct((HD, ext_counts.shape[1] * BS), jnp.bfloat16),
         ],
         in_specs=[smem, smem, vmem, pl.BlockSpec(memory_space=pl.ANY)],
         out_specs=[vmem] * 4,
@@ -696,7 +751,7 @@
             pltpu.VMEM((rows, width), jnp.bfloat16), pltpu.SemaphoreType.DMA((3, blocks)),
         ],
         name="unpack_blocks",
-    )(slot_table, ext_counts, ext_counts.reshape(1, -1), made)
+    )(slot_table, ext_counts, ext_counts, made)
 
 
 def patch_kernel(
@@ -875,7 +930,7 @@
             halo(a, which).wait_send()
 
 
-def attend_patches(q, k, vt, valid, w_proj, b_proj, regions, tile=256, group=4, chunk=256):
+def attend_patches(q, k, vt, valid, w_proj, b_proj, regions, tile=512, group=4, chunk=256):
     rows, width = q.shape
     half = rows // 2
     heads = width // HD
@@ -919,6 +974,15 @@
     slots = max(2, 2 * blocks // regions)
     half_rows = PATCH // 2
     half_blocks = half_rows // BS
+
+    if heads_axis == 2:
+        send = gather_blocks(points, hilbert_pos, regions, slots, heads_axis)
+        made, slot_table, ext_counts = swap(
+            send, hilbert_pos, counts, ln_gain, ln_bias, jnp.transpose(w_qkv, (1, 0, 2)), b_qkv,
+            regions, slots, blocks, half_blocks,
+        )
+        q, k, vt, flags = unpack_blocks(made, slot_table, ext_counts, blocks)
+        return attend_patches(q, k, vt, flags, w_proj, b_proj, regions)
 
     position = jnp.arange(blocks, dtype=jnp.int32)
     my_dest = lax.dynamic_slice_in_dim(hilbert_pos, r * blocks, blocks) // blocks
@@ -958,14 +1022,6 @@
     pad = width - group_width
     valid = valid_ext[half_rows:half_rows + rows]
     w_out = jnp.pad(w_proj, ((0, pad), (0, 0)))
-    if heads_axis == 2:
-        send = gather_blocks(points, hilbert_pos, regions, slots, heads_axis)
-        made = swap(
-            send, ln_gain, ln_bias, jnp.transpose(w_qkv, (1, 0, 2)), b_qkv, regions
-        )
-        q, k, vt, flags = unpack_blocks(made, slot_table, ext_counts)
-        return attend_patches(q, k, vt, flags, w_proj, b_proj, regions)
-
     packed = pack_blocks(points, ln_gain, ln_bias, h, pack_table, heads_axis)
     recv = exchange(packed, regions, heads_axis)
     weight = jnp.pad(w_qkv, ((0, 0), (0, 0), (0, pad))).reshape(model_width, 3 * width)

time: 83.2 us -> 77 us (0.925)
  other arithmetic: 3.82 us -> 0 us
  Pallas kernels: 77 us -> 74.7 us
    pallas_call x1, Pallas kernels: 30.7 us -> 27.7 us  [attend_patches(): pl.pallas_call(functools.partial(patch_kernel, regions, tile, group, chun...]
    reduce_sum x3 -> x0, other arithmetic: 1.77 us -> none  [the longest x1 1.47 us: shards(): jnp.sum(jnp.where(here, counts[None, :], 0), axis=1, dtype=jnp.int32)]
    eq x2 -> x0, other arithmetic: 1.46 us -> none  [the longest x1 0.76 us: shards(): here = hilbert_pos[None, :] == ext[:, None]]
where the time goes in v4:
time: 77 us; the launch traced here: 76.6 us
  Pallas kernels  74.7 us (97%)
  local copies, waits for them, and re-layouts  1.87 us (2%)
    pallas_call x1, Pallas kernels, swap(): pl.pallas_call(functools.partial(swap_kernel, regions, regions // 4, (slo...  39.4 us
    pallas_call x1, Pallas kernels, attend_patches(): pl.pallas_call(functools.partial(patch_kernel, regions, tile, group, chun...  27.7 us
    pallas_call x1, Pallas kernels, unpack_blocks(): pl.pallas_call(unpack_kernel, out_shape=[jax.ShapeDtypeStruct((rows, widt...  4.81 us
    pallas_call x1, Pallas kernels, gather_blocks(): pl.pallas_call(functools.partial(gather_kernel, slots), out_shape=jax.Sha...  2.84 us
    unnamed x1, local copies, waits for them, and re-layouts  1.87 us

profile of v4, /device:TPU:0, one launch (start us, length us, event | category | flops | bytes accessed | tf_op | source)
XLA Modules:
  0.0 76.6 jit_solution(15900981850508321911)
XLA Ops:
  0.0 2.8 %gather_blocks.1.send = bf16[2,2048,256]{2,1,0:T(8,128)(2,1)} custom-call(s32[512]{0:T(512)} %pos_ref.1, bf16[1024,512]{1,0:T(8,128)(2,1)} %x_ref.1), custom_call_target="tpu_custom_call" | custom-call | tf_op jit(solution)/shard_map/gather_blocks/pallas_call | solution.py:412
  2.8 39.4 %swap.1 = (bf16[2048,768]{1,0:T(8,128)(2,1)}, s32[1,64]{1,0:T(1,128)}, s32[1,64]{1,0:T(1,128)}) custom-call(bf16[2,2048,256]{2,1,0:T(8,128)(2,1)} %gather_blocks.1.send, s32[1,512]{1,0:T(1,128)} %bitcast.7, s32[1,512]{1,0:T(1,128)} %bitcast.8, f32[1,512]{1,0:T(1,128)} %bitcast.9, f32[1,512]{1,0:T(1,128)} %bitcast.10, bf16[3,512,256]{2,1,0:T(8,128)(2,1)} %bitcast.6, ...), custom_call_target="tpu_custom_call" | custom-call | tf_op jit(solution)/shard_map/swap/pallas_call | solution.py:646
  42.2 4.8 %unpack_blocks.1 = (bf16[1024,256]{1,0:T(8,128)(2,1)}, bf16[1024,256]{1,0:T(8,128)(2,1)}, bf16[256,1024]{1,0:T(8,128)(2,1)}, bf16[16,2048]{1,0:T(8,128)(2,1)}) custom-call(s32[1,64]{1,0:T(1,128)} %get-tuple-element.12.slot_ref, s32[1,64]{1,0:T(1,128)} %get-tuple-element.13.count_ref.ext_ref, s32[1,64]{1,0:T(1,128)} %get-tuple-element.13.count_ref.ext_ref, ...), custom_call_target="tpu_custom_call" | custom-call | tf_op jit(solution)/shard_map/unpack_blocks/pallas_call | solution.py:740
  47.0 27.7 %attend_patches.1 = bf16[512,512]{1,0:T(8,128)(2,1)} custom-call(bf16[1024,256]{1,0:T(8,128)(2,1)} %get-tuple-element.15.q_ref, bf16[1024,256]{1,0:T(8,128)(2,1)} %get-tuple-element.16.k_ref, bf16[256,1024]{1,0:T(8,128)(2,1)} %get-tuple-element.17.vt_ref, bf16[16,2048]{1,0:T(8,128)(2,1)} %get-tuple-element.18.valid_ref, bf16[256,512]{1,0:T(8,128)(2,1)} %w_ref.1, ...), custom_call_target="tpu_custom_call" | custom-call | tf_op jit(solution)/shard_map/attend_patches/pallas_call | solution.py:939
  74.7 1.9 %copy.11 = bf16[512,512]{1,0:T(8,128)(2,1)} copy(bf16[512,512]{1,0:T(8,128)(2,1)} %attend_patches.1) | data formatting | bytes 1048576

commit v5 on v4

--- a/solution.py
+++ b/solution.py
@@ -668,27 +668,23 @@
     )
 
 
-def unpack_kernel(slot_ref, count_ref, ext_ref, made, q_ref, k_ref, vt_ref, valid_ref, vals, sems):
-    blocks = q_ref.shape[0] // BS
-    width = q_ref.shape[1]
+def unpack(slot_ref, count_ref, ext_ref, made, qkv_ref, vt_ref, valid_ref):
+    blocks = qkv_ref.shape[0] // BS
+    width = vt_ref.shape[0]
     near = (ext_ref.shape[1] - blocks) // 2
-
-    def fetch(t, part, into):
-        return pltpu.make_async_copy(
-            made.at[
-                pl.ds(pl.multiple_of(slot_ref[0, near + t] * BS, BS), BS), part * width:(part + 1) * width
-            ],
-            into.at[pl.ds(pl.multiple_of(t * BS, BS), BS)],
-            sems.at[part, t],
-        )
-
-    def begin(t, carry):
-        fetch(t, 2, vals).start()
-        fetch(t, 1, k_ref).start()
-        fetch(t, 0, q_ref).start()
-        return carry
-
-    lax.fori_loop(0, blocks, begin, 0)
+    row_index = lax.broadcasted_iota(jnp.int32, (BS, width), 0)
+
+    def place(t, carry):
+        source = slot_ref[0, near + t]
+        into = pl.ds(pl.multiple_of(t * BS, BS), BS)
+        qkv_ref[into, :width] = made[source, :, :width]
+        keys = made[source, :, width:2 * width].astype(jnp.float32)
+        live = row_index < count_ref[0, near + t]
+        qkv_ref[into, width:2 * width] = jnp.where(live, keys, keys[0:1, :]).astype(jnp.bfloat16)
+        qkv_ref[into, 2 * width:] = made[source, :, 2 * width:]
+        return carry
+
+    lax.fori_loop(0, blocks, place, 0, unroll=4)
 
     total = valid_ref.shape[1]
     spread = (
@@ -698,73 +694,28 @@
     rows = valid_ref.shape[0]
     ext = jnp.broadcast_to(ext_ref[...].astype(jnp.float32), (rows, ext_ref.shape[1]))
     limit = jnp.dot(ext.astype(jnp.bfloat16), spread, preferred_element_type=jnp.float32)
-    place = (lax.broadcasted_iota(jnp.int32, (rows, total), 1) % BS).astype(jnp.float32)
-    valid_ref[...] = (place < limit).astype(jnp.float32).astype(jnp.bfloat16)
-
-    def arrive_values(t, carry):
-        fetch(t, 2, vals).wait()
-        return carry
-
-    lax.fori_loop(0, blocks, arrive_values, 0)
+    offset = (lax.broadcasted_iota(jnp.int32, (rows, total), 1) % BS).astype(jnp.float32)
+    valid_ref[...] = (offset < limit).astype(jnp.float32).astype(jnp.bfloat16)
+
     step = 256
     for i in range(blocks * BS // step):
         part = slice(i * step, (i + 1) * step)
         own = valid_ref[0:1, near * BS + i * step:near * BS + (i + 1) * step].astype(jnp.float32)
-        turned = jnp.transpose(vals[part, :].astype(jnp.float32))
+        turned = jnp.transpose(qkv_ref[part, 2 * width:].astype(jnp.float32))
         vt_ref[:, part] = (turned * own).astype(jnp.bfloat16)
-
-    row_index = lax.broadcasted_iota(jnp.int32, (BS, width), 0)
-
-    def mask(t, carry):
-        fetch(t, 1, k_ref).wait()
-        into = pl.ds(pl.multiple_of(t * BS, BS), BS)
-        keys = k_ref[into, :].astype(jnp.float32)
-        live = row_index < count_ref[0, near + t]
-        k_ref[into, :] = jnp.where(live, keys, keys[0:1, :]).astype(jnp.bfloat16)
-        return carry
-
-    lax.fori_loop(0, blocks, mask, 0, unroll=4)
-
-    def arrive_queries(t, carry):
-        fetch(t, 0, q_ref).wait()
-        return carry
-
-    lax.fori_loop(0, blocks, arrive_queries, 0)
-
-
-def unpack_blocks(made, slot_table, ext_counts, blocks):
-    width = made.shape[1] // 3
-    rows = blocks * BS
-    vmem = pl.BlockSpec(memory_space=pltpu.VMEM)
-    smem = pl.BlockSpec(memory_space=pltpu.SMEM)
-    return pl.pallas_call(
-        unpack_kernel,
-        out_shape=[
-            jax.ShapeDtypeStruct((rows, width), jnp.bfloat16),
-            jax.ShapeDtypeStruct((rows, width), jnp.bfloat16),
-            jax.ShapeDtypeStruct((width, rows), jnp.bfloat16),
-            jax.ShapeDtypeStruct((HD, ext_counts.shape[1] * BS), jnp.bfloat16),
-        ],
-        in_specs=[smem, smem, vmem, pl.BlockSpec(memory_space=pl.ANY)],
-        out_specs=[vmem] * 4,
-        scratch_shapes=[
-            pltpu.VMEM((rows, width), jnp.bfloat16), pltpu.SemaphoreType.DMA((3, blocks)),
-        ],
-        name="unpack_blocks",
-    )(slot_table, ext_counts, ext_counts, made)
 
 
 def patch_kernel(
     regions, tile, group, chunk,
-    q_ref, k_ref, vt_ref, valid_ref, w_ref, b_ref, out_ref,
-    kh, vth, w_other, acc, peaks, att, att_in, ahead, ahead_peak,
+    slot_ref, count_ref, ext_ref, made, w_ref, b_ref, out_ref,
+    qkv_ref, vt_ref, valid_ref, kh, vth, w_other, acc, peaks, att, att_in, ahead, ahead_peak,
     send_sem, recv_sem, side_sem,
 ):
     r = lax.axis_index("region")
     h = lax.axis_index("head")
     other = 1 - h
     half = kh.shape[1]
-    width = q_ref.shape[1]
+    width = kh.shape[2]
     heads = width // HD
     per = LANES // HD
     tiles = half // tile
@@ -780,6 +731,7 @@
             barrier, inc=1, device_id={"region": toward(a)}, device_id_type=MESH
         )
     pl.semaphore_signal(barrier, inc=1, device_id={"head": other}, device_id_type=MESH)
+    unpack(slot_ref, count_ref, ext_ref, made, qkv_ref, vt_ref, valid_ref)
     pl.semaphore_wait(barrier, 3)
 
     def start_of(a):
@@ -787,7 +739,7 @@
 
     def halo(a, which):
         rows = pl.ds(start_of(1 - a), half)
-        source = k_ref.at[rows, :] if which == 0 else vt_ref.at[:, rows]
+        source = qkv_ref.at[rows, width:2 * width] if which == 0 else vt_ref.at[:, rows]
         target = kh.at[a] if which == 0 else vth.at[a]
         return pltpu.make_async_remote_copy(
             src_ref=source, dst_ref=target,
@@ -810,13 +762,14 @@
     weights.start()
 
     def score(slot, a, n, i, keys):
-        columns = pl.ds(pl.multiple_of(n // per * LANES, LANES), LANES)
+        column = pl.multiple_of(n // per * LANES, LANES)
+        columns = pl.ds(column, LANES)
         mine = (lane // HD == n % per).astype(jnp.float32).astype(jnp.bfloat16)
-        queries = q_ref[pl.ds(pl.multiple_of(a * half + i * tile, tile), tile), columns] * mine
+        queries = qkv_ref[pl.ds(pl.multiple_of(a * half + i * tile, tile), tile), columns] * mine
         top = None
         for first in range(0, half, chunk):
             scores = lax.dot_general(
-                keys(a, first, columns), queries, (((1,), (1,)), ((), ())),
+                keys(a, first, column), queries, (((1,), (1,)), ((), ())),
                 preferred_element_type=jnp.float32,
             )
             ahead[slot, first:first + chunk] = scores
@@ -852,8 +805,9 @@
 
         lax.fori_loop(trip_from, trip_to, body, 0)
 
-    def near_keys(a, first, columns):
-        return k_ref[pl.ds(pl.multiple_of(a * half + first, chunk), chunk), columns]
+    def near_keys(a, first, column):
+        columns = pl.ds(pl.multiple_of(width + column, LANES), LANES)
+        return qkv_ref[pl.ds(pl.multiple_of(a * half + first, chunk), chunk), columns]
 
     def near_vals(a, rows, first):
         return vt_ref[rows, pl.ds(pl.multiple_of(a * half + first, chunk), chunk)]
@@ -861,8 +815,8 @@
     def near_flags(a, first):
         return valid_ref[:, pl.ds(pl.multiple_of((a + 1) * half + first, chunk), chunk)]
 
-    def far_keys(a, first, columns):
-        return kh[a, first:first + chunk, columns]
+    def far_keys(a, first, column):
+        return kh[a, first:first + chunk, pl.ds(column, LANES)]
 
     def far_vals(a, rows, first):
         return vth[a, rows, first:first + chunk]
@@ -930,8 +884,11 @@
             halo(a, which).wait_send()
 
 
-def attend_patches(q, k, vt, valid, w_proj, b_proj, regions, tile=512, group=4, chunk=256):
-    rows, width = q.shape
+def attend_patches(made, slots, counts, w_proj, b_proj, regions, blocks, tile=512, group=4, chunk=256):
+    width = made.shape[1] // 3
+    rows = blocks * BS
+    span = counts.shape[1] * BS
+    smem = pl.BlockSpec(memory_space=pltpu.SMEM)
     half = rows // 2
     heads = width // HD
     columns = w_proj.shape[1]
@@ -939,9 +896,12 @@
     return pl.pallas_call(
         functools.partial(patch_kernel, regions, tile, group, chunk),
         out_shape=jax.ShapeDtypeStruct((half, columns), jnp.bfloat16),
-        in_specs=[vmem] * 6,
+        in_specs=[smem, smem] + [vmem] * 4,
         out_specs=vmem,
         scratch_shapes=[
+            pltpu.VMEM((rows, 3 * width), jnp.bfloat16),
+            pltpu.VMEM((width, rows), jnp.bfloat16),
+            pltpu.VMEM((HD, span), jnp.bfloat16),
             pltpu.VMEM((2, half, width), jnp.bfloat16),
             pltpu.VMEM((2, width, half), jnp.bfloat16),
             pltpu.VMEM((width, columns), jnp.bfloat16),
@@ -957,7 +917,7 @@
         ],
         compiler_params=pltpu.CompilerParams(collective_id=2, has_side_effects=True),
         name="attend_patches",
-    )(q, k, vt, valid, w_proj, b_proj.reshape(1, -1))
+    )(slots, counts, counts, made.reshape(-1, BS, 3 * width), w_proj, b_proj.reshape(1, -1))
 
 
 def shards(points, ln_gain, ln_bias, w_qkv, b_qkv, w_proj, b_proj, counts, hilbert_pos):
@@ -981,8 +941,7 @@
             send, hilbert_pos, counts, ln_gain, ln_bias, jnp.transpose(w_qkv, (1, 0, 2)), b_qkv,
             regions, slots, blocks, half_blocks,
         )
-        q, k, vt, flags = unpack_blocks(made, slot_table, ext_counts, blocks)
-        return attend_patches(q, k, vt, flags, w_proj, b_proj, regions)
+        return attend_patches(made, slot_table, ext_counts, w_proj, b_proj, regions, blocks)
 
     position = jnp.arange(blocks, dtype=jnp.int32)
     my_dest = lax.dynamic_slice_in_dim(hilbert_pos, r * blocks, blocks) // blocks

time: 77 us -> 72.8 us (0.945)
  Pallas kernels: 74.7 us -> 70.6 us
    pallas_call x1 -> x0, Pallas kernels: 4.81 us -> none  [unpack_blocks(): pl.pallas_call(unpack_kernel, out_shape=[jax.ShapeDtypeStruct((rows, widt...]
    pallas_call x1, Pallas kernels: 27.7 us -> 28.5 us  [attend_patches(): pl.pallas_call(functools.partial(patch_kernel, regions, tile, group, chun...]
where the time goes in v5:
time: 72.8 us; the launch traced here: 72.5 us
  Pallas kernels  70.6 us (97%)
  local copies, waits for them, and re-layouts  1.87 us (3%)
    pallas_call x1, Pallas kernels, swap(): pl.pallas_call(functools.partial(swap_kernel, regions, regions // 4, (slo...  39.3 us
    pallas_call x1, Pallas kernels, attend_patches(): pl.pallas_call(functools.partial(patch_kernel, regions, tile, group, chun...  28.5 us
    pallas_call x1, Pallas kernels, gather_blocks(): pl.pallas_call(functools.partial(gather_kernel, slots), out_shape=jax.Sha...  2.84 us
    unnamed x1, local copies, waits for them, and re-layouts  1.87 us

profile of v5, /device:TPU:0, one launch (start us, length us, event | category | flops | bytes accessed | tf_op | source)
XLA Modules:
  0.0 72.5 jit_solution(6704115037626929565)
XLA Ops:
  0.0 2.8 %gather_blocks.1.send = bf16[2,2048,256]{2,1,0:T(8,128)(2,1)} custom-call(s32[512]{0:T(512)} %pos_ref.1, bf16[1024,512]{1,0:T(8,128)(2,1)} %x_ref.1), custom_call_target="tpu_custom_call" | custom-call | tf_op jit(solution)/shard_map/gather_blocks/pallas_call | solution.py:412
  2.8 39.3 %swap.1 = (bf16[2048,768]{1,0:T(8,128)(2,1)}, s32[1,64]{1,0:T(1,128)}, s32[1,64]{1,0:T(1,128)}) custom-call(bf16[2,2048,256]{2,1,0:T(8,128)(2,1)} %gather_blocks.1.send, s32[1,512]{1,0:T(1,128)} %bitcast.9, s32[1,512]{1,0:T(1,128)} %bitcast.11, f32[1,512]{1,0:T(1,128)} %bitcast.12, f32[1,512]{1,0:T(1,128)} %bitcast.13, bf16[3,512,256]{2,1,0:T(8,128)(2,1)} %bitcast.8, ...), custom_call_target="tpu_custom_call" | custom-call | tf_op jit(solution)/shard_map/swap/pallas_call | solution.py:646
  42.1 28.5 %attend_patches.1 = bf16[512,512]{1,0:T(8,128)(2,1)} custom-call(s32[1,64]{1,0:T(1,128)} %get-tuple-element.8.slot_ref, s32[1,64]{1,0:T(1,128)} %get-tuple-element.9.count_ref.ext_ref, s32[1,64]{1,0:T(1,128)} %get-tuple-element.9.count_ref.ext_ref, bf16[64,32,768]{2,1,0:T(8,128)(2,1)} %bitcast.7, bf16[256,512]{1,0:T(8,128)(2,1)} %w_ref.1, f32[1,512]{1,0:T(1,128)} %bitcast.10), custom_call_target="tpu_custom_call" | custom-call | tf_op jit(solution)/shard_map/attend_patches/pallas_call | solution.py:896
  70.6 1.9 %copy.11 = bf16[512,512]{1,0:T(8,128)(2,1)} copy(bf16[512,512]{1,0:T(8,128)(2,1)} %attend_patches.1) | data formatting | bytes 1048576
